TPU v7x, 32 devices: a whole 2x2x4 slice. The times are simulated.
32 devices in a mesh: cplx: 4 (over y, core), dap: 8 (over z, x).
Axes of the slice: x: 2, y: 2, z: 4, core: 2. Of those that a mesh axis runs over, the one named last changes fastest.
Arguments:
- alignment_features: bfloat16 [64, 64, 256], P(('cplx', 'dap')), parts along dimension 0, may hold values from -6 to 6
- couple_features: bfloat16 [256, 64, 128], P(('cplx', 'dap')), parts along dimension 0, may hold values from -6 to 6
- alignment_presence: int32 [64, 64], P('cplx'), parts along dimension 0, may hold values 0 or 1
- amino_presence: int32 [256], P('cplx'), parts along dimension 0, may hold values 0 or 1
- strand_identity: int32 [256], P('cplx'), parts along dimension 0, may hold values from 0 to 3, never falling along the last dimension, each value on 1 to 32 neighbouring positions
- strand_couple_embedding: float32 [2, 128], replicated, may hold values from -4 to 4
- fourfold_input_matrix: bfloat16 [256, 1024], replicated, may hold values from -0.375 to 0.375
- heads_merge_matrix: bfloat16 [256, 256], replicated, may hold values from -1.5 to 1.5
- couple_logit_matrix: bfloat16 [128, 8], replicated, may hold values from -30 to 30
- twin_factor_matrix: bfloat16 [256, 64], replicated, may hold values from -0.375 to 0.375
- tensor_reduce_matrix: bfloat16 [1024, 128], replicated, may hold values from -0.75 to 0.75
Outputs:
- alignment_mixed: bfloat16 [64, 64, 256], P(('cplx', 'dap')), parts along dimension 0
- couple_refreshed: bfloat16 [256, 64, 128], P(('cplx', 'dap')), parts along dimension 0
There are 4 independent parts, one for each index of `cplx`. A program takes and returns all parts, laid end to end along the dimension named above; an argument that names none is the same for every part. Nothing has to cross between parts.
All inputs are finite; a program needn't handle non-finite values.
Results may differ from a plain program's by a relative error of at most 0.0075.
The roundings to bfloat16 on the way count: a program that leaves them out, or rounds other values in their place, can miss the bound.
Values may be sent and summed in bfloat16 or wider, within the bound.
No kernel may reach another device: no remote copies, remote signals or barrier semaphores. Data moves between devices by JAX's collectives and lax.ppermute only.
A program may use at most 64 MiB of HBM per device.

v0:
```python
import jax
import jax.numpy as jnp
from jax import lax
from jax.sharding import PartitionSpec as P

EPS = 1e-05


def standardize_features(x):
    x = x.astype(jnp.float32)
    center = x - jnp.mean(x, axis=-1, keepdims=True)
    spread = jnp.mean(center * center, axis=-1, keepdims=True)
    return center * lax.rsqrt(spread + EPS)


def on_device(
    alignment_features,
    couple_features,
    alignment_presence,
    amino_presence,
    strand_identity,
    strand_couple_embedding,
    fourfold_input_matrix,
    heads_merge_matrix,
    couple_logit_matrix,
    twin_factor_matrix,
    tensor_reduce_matrix,
):
    res_here = couple_features.shape[0]
    every_amino_line = couple_features.shape[1]
    device_aligned_lines = alignment_features.shape[0]
    width = twin_factor_matrix.shape[1] // 2
    head_count = couple_logit_matrix.shape[1]
    head_size = heads_merge_matrix.shape[0] // head_count
    position = lax.axis_index("dap")
    res_start = position * res_here
    seq_start = position * device_aligned_lines
    chain_here = lax.dynamic_slice_in_dim(strand_identity, res_start, res_here)
    same = (chain_here[:, None] == strand_identity[None, :]).astype(jnp.float32)[..., None]
    z_in = (
        couple_features.astype(jnp.float32)
        + (1.0 - same) * strand_couple_embedding[0]
        + same * strand_couple_embedding[1]
    )
    pair_ln = standardize_features(z_in).astype(jnp.bfloat16)
    bias_here = jnp.einsum(
        "ijc,ch->hij", pair_ln, couple_logit_matrix, preferred_element_type=jnp.float32
    ).astype(jnp.bfloat16)
    bias_all = lax.all_gather(bias_here, "dap", axis=1, tiled=True)
    presence_numeric = alignment_presence.astype(jnp.float32)
    mask_rows = lax.dynamic_slice_in_dim(presence_numeric, seq_start, device_aligned_lines, 0)
    standardized_alignment = standardize_features(alignment_features).astype(jnp.bfloat16)
    mapped_lines = jnp.dot(
        standardized_alignment.reshape(
            device_aligned_lines * every_amino_line, alignment_features.shape[2]
        ),
        fourfold_input_matrix,
        preferred_element_type=jnp.float32,
    )
    mapped_lines = mapped_lines.reshape(
        device_aligned_lines, every_amino_line, 4, head_count, head_size
    )
    asking_vectors = (mapped_lines[:, :, 0] * head_size ** (-0.5)).astype(jnp.bfloat16)
    target_vectors = mapped_lines[:, :, 1].astype(jnp.bfloat16)
    content_vectors = mapped_lines[:, :, 2].astype(jnp.bfloat16)
    sigmoid_factors = jax.nn.sigmoid(mapped_lines[:, :, 3])
    scores = jnp.einsum(
        "sihd,sjhd->shij", asking_vectors, target_vectors, preferred_element_type=jnp.float32
    )
    scores = (
        scores
        + bias_all.astype(jnp.float32)[None]
        + ((mask_rows - 1.0) * 1000000000.0)[:, None, None, :]
    )
    weights = jax.nn.softmax(scores, axis=-1).astype(jnp.bfloat16)
    context = jnp.einsum(
        "shij,sjhd->sihd", weights, content_vectors, preferred_element_type=jnp.float32
    )
    gated_values = (
        (sigmoid_factors * context)
        .astype(jnp.bfloat16)
        .reshape(device_aligned_lines * every_amino_line, head_count * head_size)
    )
    offset_lines = jnp.dot(
        gated_values, heads_merge_matrix, preferred_element_type=jnp.float32
    ).reshape(alignment_features.shape)
    alignment_mixed = (alignment_features.astype(jnp.float32) + offset_lines).astype(jnp.bfloat16)
    mask_cols = lax.dynamic_slice_in_dim(presence_numeric, res_start, res_here, 1)
    count = jnp.dot(mask_cols.T, presence_numeric, precision=lax.Precision.HIGHEST) + 1.0
    rows_ln = standardize_features(alignment_mixed).astype(jnp.bfloat16)
    twin_factor_features = jnp.einsum(
        "sjm,mk->jsk", rows_ln, twin_factor_matrix, preferred_element_type=jnp.float32
    )
    mask_t = mask_rows.T[..., None]
    left_rows = (
        (twin_factor_features[:, :, :width] * mask_t)
        .astype(jnp.bfloat16)
        .reshape(every_amino_line, device_aligned_lines * width)
    )
    right_rows = (
        (twin_factor_features[:, :, width:] * mask_t)
        .astype(jnp.bfloat16)
        .reshape(every_amino_line, device_aligned_lines * width)
    )
    left_full = lax.all_to_all(left_rows, "dap", split_axis=0, concat_axis=1, tiled=True)
    piece = lax.all_gather(right_rows, "dap", axis=1, tiled=True)
    columns = piece.shape[1]
    left_part = left_full.reshape(res_here, columns // width, width)
    right_part = piece.reshape(every_amino_line, columns // width, width)
    outer = jnp.einsum("isc,jse->ijce", left_part, right_part, preferred_element_type=jnp.float32)
    outer = outer.astype(jnp.bfloat16).reshape(res_here, every_amino_line, width * width)
    update = (
        jnp.einsum("ijk,kz->ijz", outer, tensor_reduce_matrix, preferred_element_type=jnp.float32)
        / count[..., None]
    )
    resf = amino_presence.astype(jnp.float32)
    res_local = lax.dynamic_slice_in_dim(resf, res_start, res_here)
    pair_mask = res_local[:, None] * resf[None, :]
    couple_refreshed = (z_in + pair_mask[..., None] * update).astype(jnp.bfloat16)
    return (alignment_mixed, couple_refreshed)


def solution(mesh):
    in_specs = (
        P(("cplx", "dap"), None, None),
        P(("cplx", "dap"), None, None),
        P("cplx", None),
        P("cplx"),
        P("cplx"),
        P(),
        P(),
        P(),
        P(),
        P(),
        P(),
    )
    out_specs = (P(("cplx", "dap"), None, None), P(("cplx", "dap"), None, None))
    return jax.shard_map(
        on_device, mesh=mesh, in_specs=in_specs, out_specs=out_specs, check_vma=False
    )
```

profile of v0, /device:TPU:0, one launch (start us, length us, event | category | flops | bytes accessed | tf_op | source)
XLA Modules:
  0.0 88.1 jit_solution(13455693065240458379)
XLA Ops:
  0.6 0.0 copy-start
  0.6 0.0 copy-start.1
  0.7 0.8 dynamic_slice.12
  1.4 0.7 broadcast_subtract_fusion
  2.2 0.7 compare_convert_fusion
  2.9 0.9 %convert_reduce_fusion = f32[2,64]{1,0:T(2,128)S(1)} fusion(bf16[2,64,256]{2,1,0:T(8,128)(2,1)} %param.11), kind=kLoop, calls=%fused_computation.35 | loop fusion | flops 65408 | bytes 66048 | tf_op jit(solution)/shard_map/reduce_sum | solution.py:11
  3.8 1.0 %fusion.24 = f32[2,64]{1,0:T(2,128)S(1)} fusion(bf16[2,64,256]{2,1,0:T(8,128)(2,1)} %param.11, f32[2,64]{1,0:T(2,128)S(1)} %broadcast_multiply_fusion.3), kind=kLoop, calls=%fused_computation.42 | loop fusion | flops 130944 | bytes 66560 | tf_op jit(solution)/shard_map/reduce_sum | solution.py:12
  4.9 0.8 slice_bitcast_fusion.5
  5.6 1.2 %fusion.19 = f32[8,64]{1,0:T(8,128)S(1)} fusion(bf16[8,64,128]{2,1,0:T(8,128)(2,1)} %param.12, f32[128]{0:T(128)S(1)} %get-tuple-element.7, f32[8,64]{1,0:T(8,128)S(1)} %compare_convert_fusion, f32[128]{0:T(128)S(1)} %get-tuple-element.6, f32[8,64]{1,0:T(8,128)S(1)} %broadcast_subtract_fusion), kind=kLoop, calls=%fused_computation.33 | loop fusion | flops 392704 | bytes 138240 | tf_op jit(solution)/shard_map/reduce_sum | solution.py:11
  6.9 1.3 %multiply_reduce_fusion = f32[8,64]{1,0:T(8,128)S(1)} fusion(bf16[8,64,128]{2,1,0:T(8,128)(2,1)} %param.12, f32[8,64]{1,0:T(8,128)S(1)} %broadcast_multiply_fusion.1, f32[128]{0:T(128)S(1)} %get-tuple-element.7, f32[8,64]{1,0:T(8,128)S(1)} %compare_convert_fusion, f32[128]{0:T(128)S(1)} %get-tuple-element.6, f32[8,64]{1,0:T(8,128)S(1)} %broadcast_subtract_fusion), kind=kLoop, calls=%fused_computation.30 | loop fusion | flops 523776 | bytes 140288 | tf_op jit(solution)/shard_map/reduce_sum | solution.py:12
  8.2 0.7 convert_element_type.94
  8.9 1.4 %fusion.10 = bf16[8,8,64]{2,0,1:T(8,128)(2,1)S(1)} fusion(bf16[8,64,128]{2,1,0:T(8,128)(2,1)} %param.12, f32[8,64]{1,0:T(8,128)S(1)} %add_rsqrt_fusion, f32[8,64]{1,0:T(8,128)S(1)} %broadcast_multiply_fusion.1, f32[128]{0:T(128)S(1)} %get-tuple-element.7, f32[8,64]{1,0:T(8,128)S(1)} %compare_convert_fusion, f32[128]{0:T(128)S(1)} %get-tuple-element.6, ...), kind=kOutput, calls=%fused_computation.17 | convolution fusion | flops 1576960 | bytes 150528 | tf_op jit(solution)/shard_map/ijc,ch->hij/dot_general | solution.py:46
  10.2 32.3 %all_gather.6 = bf16[8,64,64]{2,0,1:T(8,128)(2,1)S(1)} all-gather(bf16[8,8,64]{2,0,1:T(8,128)(2,1)S(1)} %fusion.10), channel_id=1, replica_groups=mesh['cplx'=4,'dap'=8] {'dap'}, dimensions={1}, use_global_device_ids=true | all-gather | bytes 73728 | tf_op jit(solution)/shard_map/all_gather | solution.py:49
  42.6 0.1 copy.28
  42.7 1.2 %copy.27 = bf16[256,1024]{0,1:T(8,128)(2,1)S(1)} copy(bf16[256,1024]{1,0:T(8,128)(2,1)} %param.17) | data formatting | bytes 1048576 | tf_op args[6]
  44.0 0.0 copy-done.1
  44.0 0.4 fusion.49
  44.4 0.3 fusion.3
  44.7 0.0 copy-start.4
  44.7 0.1 fusion.50
  44.8 0.0 copy-start.5
  44.8 0.0 copy-start.6
  44.9 0.2 fusion.7
  45.1 0.5 copy-done.4
  45.6 0.3 convert_reduce_fusion.1
  45.9 0.0 copy-start.3
  45.9 0.2 fusion.26
  46.1 0.0 copy-done.5
  46.1 0.2 convolution_bitcast_fusion.1
  46.3 0.1 copy.31
  46.4 0.1 all_to_all.12
  46.5 0.7 reshape.178
  47.2 5.5 %all-to-all-start = ((bf16[8,2,256]{2,1,0:T(2,128)(2,1)}), bf16[8,2,256]{2,1,0:T(2,128)(2,1)S(1)}, u32[]{:S(2)}, u32[]{:S(2)}) async-start(bf16[8,2,256]{2,1,0:T(2,128)(2,1)} %reshape.178), calls=%async_computation | async-start | bytes 16384 | tf_op jit(solution)/shard_map/all_to_all | solution.py:105
  52.7 0.3 convolution_add_fusion.2
  53.0 0.0 copy-done.6
  53.0 0.1 dynamic_slice.14
  53.1 0.1 broadcast_multiply_fusion
  53.1 31.1 %all_gather.7 = bf16[64,512]{0,1:T(8,128)(2,1)S(1)} all-gather(bf16[64,64]{0,1:T(8,128)(2,1)S(1)} %bitcast.75), channel_id=1, replica_groups=mesh['cplx'=4,'dap'=8] {'dap'}, dimensions={1}, use_global_device_ids=true | all-gather | bytes 73728 | tf_op jit(solution)/shard_map/all_gather | solution.py:106
  84.2 0.0 all-to-all-done
  84.2 0.1 reshape.179
  84.3 0.1 reshape.175
  84.4 0.7 convert_bitcast_fusion
  85.1 0.0 copy-start.2
  85.1 1.4 %copy.34 = bf16[8,64,32,32]{1,3,2,0:T(8,128)(2,1)S(1)} copy(bf16[8,64,32,32]{1,2,0,3:T(8,128)(2,1)S(1)} %convert_bitcast_fusion) | data formatting | bytes 2097152 | tf_op jit(solution)/shard_map/convert_element_type | solution.py:111
  86.5 0.0 copy-done.3
  86.5 0.0 copy-done
  86.5 0.0 copy-done.2
  86.5 1.6 %fusion.8 = bf16[8,64,128]{2,1,0:T(8,128)(2,1)} fusion(bf16[8,64,1024]{1,2,0:T(8,128)(2,1)S(1)} %bitcast.72, bf16[1024,128]{1,0:T(8,128)(2,1)S(1)} %copy-done, bf16[8,64,128]{2,1,0:T(8,128)(2,1)S(1)} %copy-done.2, f32[8,64]{1,0:T(8,128)S(1)} %convolution_add_fusion.2, f32[8,64]{1,0:T(8,128)S(1)} %broadcast_multiply_fusion, f32[128]{0:T(128)S(1)} %get-tuple-element.7, ...), kind=kOutput, calls=%fused_computation.12 | convolution fusion | flops 134807552 | bytes 1582080 | tf_op jit(solution)/shard_map/ijk,kz->ijz/dot_general | solution.py:113
  (10 shorter events, 0.1 us)
Async XLA Ops:
  0.6 85.9 %copy-start = (bf16[1024,128]{1,0:T(8,128)(2,1)S(1)}, bf16[1024,128]{1,0:T(8,128)(2,1)}, u32[]{:S(2)}) copy-start(bf16[1024,128]{1,0:T(8,128)(2,1)} %param.21) | copy-start | bytes 786436
  0.6 43.3 %copy-start.1 = (bf16[2,64,256]{2,1,0:T(8,128)(2,1)S(1)}, bf16[2,64,256]{2,1,0:T(8,128)(2,1)}, u32[]{:S(2)}) copy-start(bf16[2,64,256]{2,1,0:T(8,128)(2,1)} %param.11) | copy-start | bytes 196612
  44.7 0.9 %copy-start.4 = (bf16[256,256]{1,0:T(8,128)(2,1)S(1)}, bf16[256,256]{1,0:T(8,128)(2,1)}, u32[]{:S(2)}) copy-start(bf16[256,256]{1,0:T(8,128)(2,1)} %param.18) | copy-start | bytes 393220
  44.8 1.2 %copy-start.5 = (bf16[256,64]{0,1:T(8,128)(2,1)S(1)}, bf16[256,64]{0,1:T(8,128)(2,1)}, u32[]{:S(2)}) copy-start(bf16[256,64]{0,1:T(8,128)(2,1)} %param.20) | copy-start | bytes 98308
  44.8 8.1 %copy-start.6 = (s32[64]{0:T(128)S(1)}, s32[64]{0:T(128)}, u32[]{:S(2)}) copy-start(s32[64]{0:T(128)} %param.14) | copy-start | bytes 772
  45.9 40.6 %copy-start.3 = (bf16[2,64,256]{2,1,0:T(8,128)(2,1)}, bf16[2,64,256]{2,1,0:T(8,128)(2,1)S(1)}, u32[]{:S(2)}) copy-start(bf16[2,64,256]{2,1,0:T(8,128)(2,1)S(1)} %get-tuple-element.11) | copy-start | bytes 196612
  47.2 37.0 %all-to-all-start = ((bf16[8,2,256]{2,1,0:T(2,128)(2,1)}), bf16[8,2,256]{2,1,0:T(2,128)(2,1)S(1)}, u32[]{:S(2)}, u32[]{:S(2)}) async-start(bf16[8,2,256]{2,1,0:T(2,128)(2,1)} %reshape.178), calls=%async_computation | async-start | bytes 16384 | tf_op jit(solution)/shard_map/all_to_all | solution.py:105
  85.1 1.4 %copy-start.2 = (bf16[8,64,128]{2,1,0:T(8,128)(2,1)S(1)}, bf16[8,64,128]{2,1,0:T(8,128)(2,1)}, u32[]{:S(2)}) copy-start(bf16[8,64,128]{2,1,0:T(8,128)(2,1)} %param.12) | copy-start | bytes 393220
where the time goes:
time: 88.6 us; the launch traced here: 88.1 us
  blocking collectives  63.4 us (72%)
  other arithmetic  7.06 us (8%)
  local copies, waits for them, and re-layouts  5.95 us (7%)
  starting transfers between devices  5.47 us (6%)
  matrix products  5.34 us (6%)
    all_gather x1, blocking collectives, on_device(): bias_all = lax.all_gather(bias_here, 'dap', axis=1, tiled=True)  32.3 us
    all_gather x1, blocking collectives, on_device(): piece = lax.all_gather(right_rows, 'dap', axis=1, tiled=True)  31.1 us
    all_to_all x1, starting transfers between devices, on_device(): lax.all_to_all(left_rows, 'dap', split_axis=0, concat_axis=1, tiled=True)  5.47 us
    unnamed x17, local copies, waits for them, and re-layouts  2.54 us
    reduce_sum x3, other arithmetic, standardize_features(): spread = jnp.mean(center * center, axis=-1, keepdims=True)  2.46 us
    reduce_sum x2, other arithmetic, standardize_features(): center = x - jnp.mean(x, axis=-1, keepdims=True)  2.16 us
  transfers between devices with their start and end apart: 1, of which 0 were waited for; matrix products, arithmetic and copies ran while one was open for 0% of the time, Pallas kernels for 0%

commit v1 on v0

v1 whole, which is shorter than its diff:
```python
import functools

import jax
import jax.numpy as jnp
from jax import lax
from jax.experimental import pallas as pl
from jax.experimental.pallas import tpu as pltpu
from jax.sharding import PartitionSpec as P

EPS = 1e-05
LANES = 128
F32 = jnp.float32
BF16 = jnp.bfloat16
VMEM_LIMIT = 24 * 1024 * 1024


def standardize(x):
    center = x - jnp.mean(x, axis=-1, keepdims=True)
    spread = jnp.mean(center * center, axis=-1, keepdims=True)
    return center * lax.rsqrt(spread + EPS)


def to_column(row, size):
    down = lax.broadcasted_iota(jnp.int32, (size, size), 0)
    across = lax.broadcasted_iota(jnp.int32, (size, size), 1)
    spread = jnp.where(down == across, jnp.broadcast_to(row, (size, size)), 0.0)
    return jnp.sum(spread, axis=1, keepdims=True)


def dot(a, b, contract):
    return lax.dot_general(a, b, (contract, ((), ())), preferred_element_type=F32)


NN = ((1,), (0,))
NT = ((1,), (1,))
TN = ((0,), (0,))


def pair_input(ids, ids_row, emb, x, res_start):
    rows, size, channels = x.shape
    chain = jnp.broadcast_to(to_column(ids_row[...].astype(F32), size), (size, channels))
    other, same = emb[0:1, :], emb[1:2, :]
    for i in range(rows):
        chain_i = ids[res_start + i].astype(F32)
        yield x[i].astype(F32) + jnp.where(chain == chain_i, same, other)


def bias_kernel(ids, ids_row, emb, x, logit, out):
    rows, size, _ = x.shape
    heads = logit.shape[0]
    group = heads * rows
    pack = LANES // group
    part = size // pack
    res_start = lax.axis_index("dap") * rows
    head = lax.broadcasted_iota(jnp.int32, (heads, LANES), 0)
    lane = lax.broadcasted_iota(jnp.int32, (heads, LANES), 1)
    spread = jnp.where((lane % group) // rows == head, 1.0, 0.0).astype(BF16)
    wide = dot(logit[...], spread, TN).astype(BF16)
    normed = [standardize(z).astype(BF16) for z in pair_input(ids, ids_row, emb, x, res_start)]
    full = dot(jnp.concatenate(normed, axis=0), wide, NN)
    lane = lax.broadcasted_iota(jnp.int32, (part, LANES), 1)
    total = jnp.zeros((part, LANES), F32)
    for i in range(rows):
        for half in range(pack):
            begin = i * size + half * part
            pick = (lane // group == half) & (lane % rows == i)
            total = jnp.where(pick, full[begin : begin + part, :], total)
    total = total.astype(BF16)
    for peer in range(out.shape[0]):
        out[peer] = total


def project_kernel(rows, x, weights, presence, scores, content, gate, present, present_row):
    seqs, size, depth = x.shape
    merged = content.shape[2]
    group_total = scores.shape[2]
    heads = group_total // size
    head_size = merged // heads
    seq_start = lax.axis_index("dap") * seqs
    normed = standardize(x[...].reshape(seqs * size, depth).astype(F32)).astype(BF16)
    mapped = dot(normed, weights[...], NN)
    asking = (mapped[:, :merged] * head_size**-0.5).astype(BF16).astype(F32)
    target = mapped[:, merged : 2 * merged].astype(BF16)
    content[...] = mapped[:, 2 * merged : 3 * merged].astype(BF16).reshape(content.shape)
    gate[...] = jax.nn.sigmoid(mapped[:, 3 * merged :]).reshape(gate.shape)
    lane = lax.broadcasted_iota(jnp.int32, (rows, merged), 1)
    row_pieces = []
    for s in range(seqs):
        pieces = []
        for begin in range(s * size, (s + 1) * size, rows):
            here = asking[begin : begin + rows, :]
            for h in range(heads):
                pieces.append(jnp.where(lane // head_size == h, here, 0.0))
        spread = jnp.concatenate(pieces, axis=0).astype(BF16)
        scores[s] = dot(target[s * size : (s + 1) * size, :], spread, NT)
        row = presence[pl.ds(seq_start + s, 1), :].astype(F32)
        present[s] = jnp.broadcast_to(to_column(row, size), (size, LANES))
        row_pieces.append(row)
    present_row[...] = jnp.concatenate(row_pieces, axis=1)


def attend_kernel(bias, scores, content, gate, present, present_row, x, merge, twin, mixed, out):
    devices, part, _ = bias.shape
    seqs, size, depth = x.shape
    merged = content.shape[2]
    pack = size // part
    group = LANES // pack
    rows = size // devices
    heads = group // rows
    head_size = merged // heads
    width = twin.shape[0] // 2
    lane = lax.broadcasted_iota(jnp.int32, (rows, merged), 1)
    gated = []
    tables = []
    for block in range(devices // pack):
        got = [bias[block * pack + n].astype(F32) for n in range(pack)]
        tables.append(
            jnp.concatenate(
                [
                    jnp.concatenate([g[:, half * group : (half + 1) * group] for g in got], axis=1)
                    for half in range(pack)
                ],
                axis=0,
            )
        )
    for s in range(seqs):
        absent = (present[s] - 1.0) * 1000000000.0
        context = []
        for block in range(devices // pack):
            logits = scores[s, :, block * LANES : (block + 1) * LANES] + tables[block] + absent
            raised = jnp.exp(logits - jnp.max(logits, axis=0, keepdims=True))
            weights = raised * (1.0 / jnp.sum(raised, axis=0, keepdims=True))
            mixed_heads = dot(weights.astype(BF16), content[s], TN)
            for n in range(pack):
                total = jnp.zeros((rows, merged), F32)
                for h in range(heads):
                    begin = n * group + h * rows
                    total = jnp.where(lane // head_size == h, mixed_heads[begin : begin + rows, :], total)
                context.append(total)
        gated.append((gate[s] * jnp.concatenate(context, axis=0)).astype(BF16))
    offset = dot(jnp.concatenate(gated, axis=0), merge[...], NN)
    updated = (x[...].reshape(seqs * size, depth).astype(F32) + offset).astype(BF16)
    mixed[...] = updated.reshape(mixed.shape)
    normed = standardize(updated.astype(F32)).astype(BF16)
    left = dot(normed, twin[...], NT)
    right = (dot(twin[width:, :], normed, NT) * present_row[...]).astype(BF16)
    blocks = seqs * size // LANES
    for peer in range(devices):
        for block in range(blocks):
            out[peer, block * width : (block + 1) * width, :] = right[:, block * LANES : (block + 1) * LANES]
    for peer in range(devices):
        rows_here = []
        for s in range(seqs):
            begin = peer * rows
            here = left[s * size + begin : s * size + begin + rows, :]
            rows_here.append(here * present[s, begin : begin + rows, : 2 * width])
        piece = jnp.concatenate(rows_here, axis=0)
        piece = jnp.concatenate([piece, jnp.zeros((seqs * rows, LANES - 2 * width), F32)], axis=1)
        out[peer, blocks * width :, :] = piece.astype(BF16)


def prepare_kernel(ids, amino, ids_row, amino_row, emb, x, presence, reduce, pair, scale, spread, wide):
    rows, size, channels = x.shape
    width = spread.shape[0]
    res_start = lax.axis_index("dap") * rows
    for i, z in enumerate(pair_input(ids, ids_row, emb, x, res_start)):
        pair[i] = z
    here = presence[...].astype(BF16)
    count = dot(here, here, TN)
    lane = lax.broadcasted_iota(jnp.int32, (size, size), 1)
    kept = to_column(amino_row[...].astype(F32), size)
    for i in range(rows):
        column = jnp.sum(jnp.where(lane == res_start + i, count, 0.0), axis=1, keepdims=True) + 1.0
        kept_i = amino[res_start + i].astype(F32)
        scale[i] = jnp.broadcast_to(kept * kept_i / column, (size, channels))
    wide[...] = reduce[...].astype(F32)
    for e in range(width):
        spread[:, e * channels : (e + 1) * channels] = wide[pl.ds(e, width, stride=width), :].astype(BF16)


def outer_kernel(got, spread, pair, scale, out, right_rows, left_rows):
    devices = got.shape[0]
    rows, size, channels = pair.shape
    width = spread.shape[0]
    blocks = right_rows.shape[0]
    seqs = blocks * LANES // size
    for peer in range(devices):
        for block in range(blocks):
            right_rows[block, pl.ds(peer, width, stride=devices), :] = got[
                peer, block * width : (block + 1) * width, :
            ].astype(F32)
        left_rows[pl.ds(peer, seqs * rows, stride=devices), :] = got[peer, blocks * width :, :].astype(F32)
    right = jnp.concatenate([jnp.transpose(right_rows[block]) for block in range(blocks)], axis=0).astype(BF16)
    left = left_rows[...][:, :width].astype(BF16)
    table = dot(left, spread[...], NN)
    for i in range(rows):
        update = jnp.zeros((size, channels), F32)
        for s in range(seqs):
            begin = (s * rows + i) * devices
            columns = jnp.concatenate(
                [table[begin : begin + devices, e * channels : (e + 1) * channels] for e in range(width)], axis=0
            ).astype(BF16)
            update = update + dot(right[s * size : (s + 1) * size, :], columns, NN)
        out[i] = (pair[i] + scale[i] * update).astype(BF16)


def vmem(count):
    return [pl.BlockSpec(memory_space=pltpu.VMEM) for _ in range(count)]


def smem(count):
    return [pl.BlockSpec(memory_space=pltpu.SMEM) for _ in range(count)]


def call(body, shapes, in_specs, name, flops, moved, scratch=()):
    return pl.pallas_call(
        body,
        out_shape=shapes,
        in_specs=in_specs,
        out_specs=jax.tree.map(lambda _: pl.BlockSpec(memory_space=pltpu.VMEM), shapes),
        scratch_shapes=list(scratch),
        compiler_params=pltpu.CompilerParams(vmem_limit_bytes=VMEM_LIMIT),
        cost_estimate=pl.CostEstimate(flops=flops, bytes_accessed=moved, transcendentals=0),
        name=name,
    )


def on_device(
    alignment_features,
    couple_features,
    alignment_presence,
    amino_presence,
    strand_identity,
    strand_couple_embedding,
    fourfold_input_matrix,
    heads_merge_matrix,
    couple_logit_matrix,
    twin_factor_matrix,
    tensor_reduce_matrix,
):
    rows, size, channels = couple_features.shape
    seqs, _, depth = alignment_features.shape
    devices = size // rows
    heads = couple_logit_matrix.shape[1]
    merged = heads_merge_matrix.shape[0]
    width = twin_factor_matrix.shape[1] // 2
    group = heads * rows
    pack = LANES // group
    struct = jax.ShapeDtypeStruct
    ids_row = strand_identity.reshape(1, size)
    amino_row = amino_presence.reshape(1, size)

    bias = call(
        bias_kernel,
        struct((devices, size // pack, LANES), BF16),
        smem(1) + vmem(4),
        "pair_bias",
        2 * rows * size * channels * LANES,
        2 * rows * size * channels,
    )(strand_identity, ids_row, strand_couple_embedding, couple_features, couple_logit_matrix.T)
    bias = lax.all_to_all(bias, "dap", 0, 0)

    scores, content, gate, present, present_row = call(
        functools.partial(project_kernel, rows),
        (
            struct((seqs, size, heads * size), F32),
            struct((seqs, size, merged), BF16),
            struct((seqs, size, merged), F32),
            struct((seqs, size, LANES), F32),
            struct((1, seqs * size), F32),
        ),
        vmem(3),
        "project",
        2 * seqs * size * depth * 4 * merged + 2 * seqs * size * size * heads * merged,
        2 * depth * 4 * merged,
    )(alignment_features, fourfold_input_matrix, alignment_presence)

    blocks = seqs * size // LANES
    mixed, factors = call(
        attend_kernel,
        (
            struct(alignment_features.shape, BF16),
            struct((devices, blocks * width + seqs * rows, LANES), BF16),
        ),
        vmem(9),
        "attend",
        4 * seqs * size * size * heads * merged,
        8 * seqs * size * size * heads,
    )(
        bias,
        scores,
        content,
        gate,
        present,
        present_row,
        alignment_features,
        heads_merge_matrix,
        twin_factor_matrix.T,
    )
    factors = lax.all_to_all(factors, "dap", 0, 0)

    pair, scale, spread = call(
        prepare_kernel,
        (
            struct(couple_features.shape, F32),
            struct(couple_features.shape, F32),
            struct((width, width * channels), BF16),
        ),
        smem(2) + vmem(6),
        "prepare",
        16 * rows * size * channels,
        16 * rows * size * channels,
        [pltpu.VMEM((width * width, channels), F32)],
    )(
        strand_identity,
        amino_presence,
        ids_row,
        amino_row,
        strand_couple_embedding,
        couple_features,
        alignment_presence,
        tensor_reduce_matrix,
    )

    refreshed = call(
        outer_kernel,
        struct(couple_features.shape, BF16),
        vmem(4),
        "outer_mean",
        4 * rows * size * channels * width * seqs * devices,
        16 * rows * size * channels,
        [
            pltpu.VMEM((blocks, width * devices, LANES), F32),
            pltpu.VMEM((seqs * rows * devices, LANES), F32),
        ],
    )(factors, spread, pair, scale)
    return (mixed, refreshed)


def solution(mesh):
    in_specs = (
        P(("cplx", "dap"), None, None),
        P(("cplx", "dap"), None, None),
        P("cplx", None),
        P("cplx"),
        P("cplx"),
        P(),
        P(),
        P(),
        P(),
        P(),
        P(),
    )
    out_specs = (P(("cplx", "dap"), None, None), P(("cplx", "dap"), None, None))
    return jax.shard_map(
        on_device, mesh=mesh, in_specs=in_specs, out_specs=out_specs, check_vma=False
    )
```

time: 88.6 us -> 32.1 us (0.36)
  blocking collectives: 63.4 us -> 0 us
  waiting for transfers between devices: 0.01 us -> 10.5 us
  other arithmetic: 7.06 us -> 0 us
  Pallas kernels: 0 us -> 6.24 us
  starting transfers between devices: 5.47 us -> 10.9 us
  matrix products: 5.34 us -> 0 us
  local copies, waits for them, and re-layouts: 5.95 us -> 3.28 us
    all_gather x2 -> x0, blocking collectives: 63.4 us -> none  [the longest x1 32.3 us: on_device(): bias_all = lax.all_gather(bias_here, 'dap', axis=1, tiled=True)]
    all_to_all x1 -> x2, waiting for transfers between devices: 0.01 us -> 10.5 us  [the longest x1 5.26 us: on_device(): factors = lax.all_to_all(factors, 'dap', 0, 0)]
    pallas_call x0 -> x5, Pallas kernels: none -> 6.24 us  [the longest x1 1.63 us: on_device(): call(bias_kernel, struct((devices, size // pack, LANES), BF16), smem(1) +...]
    all_to_all x1 -> x2, starting transfers between devices: 5.47 us -> 10.9 us  [the longest x1 7.41 us: on_device(): bias = lax.all_to_all(bias, 'dap', 0, 0)]
    dot_general x9 -> x0, matrix products: 5.34 us -> none  [the longest x1 1.55 us: on_device(): jnp.einsum('ijk,kz->ijz', outer, tensor_reduce_matrix, preferred_element_...]
    reduce_sum x5 -> x0, other arithmetic: 4.62 us -> none  [the longest x3 2.46 us: standardize_features(): spread = jnp.mean(center * center, axis=-1, keepdims=True)]
    convert_element_type x3 -> x0, local copies, waits for them, and re-layouts: 1.59 us -> none  [the longest x1 1.35 us: on_device(): outer.astype(jnp.bfloat16)]
    convert_element_type x4 -> x0, other arithmetic: 1.46 us -> none  [the longest x1 0.72 us: on_device(): (chain_here[:, None] == strand_identity[None, :]).astype(jnp.float32)]
  transfers between devices with their start and end apart: 1 -> 2, of which waited for: 0 -> 2; matrix products, arithmetic and copies ran while one was open for 0% -> 0% of each run, Pallas kernels for 0% -> 6%
where the time goes in v1:
time: 32.1 us; the launch traced here: 31.6 us
  starting transfers between devices  10.9 us (34%)
  waiting for transfers between devices  10.5 us (33%)
  Pallas kernels  6.24 us (19%)
  local copies, waits for them, and re-layouts  3.28 us (10%)
  between operations  0.72 us (2%)
    all_to_all x1, starting transfers between devices, on_device(): bias = lax.all_to_all(bias, 'dap', 0, 0)  7.41 us
    all_to_all x1, waiting for transfers between devices, on_device(): factors = lax.all_to_all(factors, 'dap', 0, 0)  5.26 us
    all_to_all x1, waiting for transfers between devices, on_device(): bias = lax.all_to_all(bias, 'dap', 0, 0)  5.24 us
    all_to_all x1, starting transfers between devices, on_device(): factors = lax.all_to_all(factors, 'dap', 0, 0)  3.49 us
    unnamed x24, local copies, waits for them, and re-layouts  3.28 us
    pallas_call x1, Pallas kernels, on_device(): call(bias_kernel, struct((devices, size // pack, LANES), BF16), smem(1) +...  1.63 us
    pallas_call x1, Pallas kernels, on_device(): call(attend_kernel, (struct(alignment_features.shape, BF16), struct((devi...  1.53 us
    pallas_call x1, Pallas kernels, on_device(): call(outer_kernel, struct(couple_features.shape, BF16), vmem(4), 'outer_m...  1.34 us
  transfers between devices with their start and end apart: 2, of which 2 were waited for; matrix products, arithmetic and copies ran while one was open for 0% of the time, Pallas kernels for 6%

profile of v1, /device:TPU:0, one launch (start us, length us, event | category | flops | bytes accessed | tf_op | source)
XLA Modules:
  0.0 31.6 jit_solution(7548694790085955194)
XLA Ops:
  0.6 0.0 copy-start.10
  0.6 0.0 copy-start.8
  0.7 0.0 copy-start.9
  0.7 0.7 %copy-done.10 = bf16[128,8]{0,1:T(8,128)(2,1)S(1)} copy-done((bf16[128,8]{0,1:T(8,128)(2,1)S(1)}, bf16[128,8]{0,1:T(8,128)(2,1)}, u32[]{:S(2)}) %copy-start.10) | copy-done | bytes 2072
  1.3 0.0 copy-done.8
  1.3 0.0 copy-done.9
  1.3 0.0 copy-start
  1.3 0.9 %copy-done = bf16[8,64,128]{2,1,0:T(8,128)(2,1)S(1)} copy-done((bf16[8,64,128]{2,1,0:T(8,128)(2,1)S(1)}, bf16[8,64,128]{2,1,0:T(8,128)(2,1)}, u32[]{:S(2)}) %copy-start) | copy-done | bytes 131096
  2.2 1.6 %pair_bias.1 = bf16[8,32,128]{2,1,0:T(8,128)(2,1)} custom-call(s32[64]{0:T(128)S(1)} %copy-done.8, s32[1,64]{1,0:T(1,128)S(1)} %bitcast.5, f32[2,128]{1,0:T(2,128)S(1)} %copy-done.9, bf16[8,64,128]{2,1,0:T(8,128)(2,1)S(1)} %copy-done, bf16[8,128]{1,0:T(8,128)(2,1)S(1)} %bitcast.7), custom_call_target="tpu_custom_call" | custom-call | flops 16777216 | bytes 131072 | tf_op jit(solution)/shard_map/pair_bias/pallas_call | solution.py:253
  3.9 0.0 copy-start.4
  3.9 0.0 copy-start.6
  3.9 7.4 %all-to-all-start = ((bf16[8,32,128]{2,1,0:T(8,128)(2,1)}), bf16[8,32,128]{2,1,0:T(8,128)(2,1)S(1)}, u32[]{:S(2)}, u32[]{:S(2)}) async-start(bf16[8,32,128]{2,1,0:T(8,128)(2,1)} %pair_bias.1), calls=%async_computation | async-start | bytes 131072 | tf_op jit(solution)/shard_map/all_to_all | solution.py:261
  11.3 0.0 copy-done.4
  11.3 0.0 copy-done.6
  11.3 0.0 copy-start.2
  11.3 1.0 %copy-done.2 = bf16[256,1024]{1,0:T(8,128)(2,1)S(1)} copy-done((bf16[256,1024]{1,0:T(8,128)(2,1)S(1)}, bf16[256,1024]{1,0:T(8,128)(2,1)}, u32[]{:S(2)}) %copy-start.2) | copy-done | bytes 524312
  12.4 0.0 copy-start.5
  12.4 0.0 copy-start.7
  12.4 0.6 %project.1 = (f32[2,64,512]{2,1,0:T(8,128)S(1)}, bf16[2,64,256]{2,1,0:T(8,128)(2,1)S(1)}, f32[2,64,256]{2,1,0:T(8,128)S(1)}, f32[2,64,128]{2,1,0:T(8,128)S(1)}, f32[1,128]{1,0:T(1,128)S(1)}) custom-call(bf16[2,64,256]{2,1,0:T(8,128)(2,1)S(1)} %copy-done.4, bf16[256,1024]{1,0:T(8,128)(2,1)S(1)} %copy-done.2, s32[16,64]{1,0:T(8,128)S(1)} %copy-done.6), custom_call_target="tpu_custom_call" | custom-call | flops 100663296 | bytes 524288 | tf_op jit(solution)/shard_map/project/pallas_call | solution.py:263
  13.0 5.2 %all-to-all-done.bias = bf16[8,32,128]{2,1,0:T(8,128)(2,1)S(1)} async-done(((bf16[8,32,128]{2,1,0:T(8,128)(2,1)}), bf16[8,32,128]{2,1,0:T(8,128)(2,1)S(1)}, u32[]{:S(2)}, u32[]{:S(2)}) %all-to-all-start) | async-done | bytes 65568 | tf_op jit(solution)/shard_map/all_to_all | solution.py:261
  18.2 0.0 copy-done.5
  18.2 0.0 copy-done.7
  18.2 0.0 copy-start.3
  18.2 1.5 %attend.1 = (bf16[2,64,256]{2,1,0:T(8,128)(2,1)}, bf16[8,48,128]{2,1,0:T(8,128)(2,1)}) custom-call(bf16[8,32,128]{2,1,0:T(8,128)(2,1)S(1)} %all-to-all-done.bias, f32[2,64,512]{2,1,0:T(8,128)S(1)} %get-tuple-element.12.scores, bf16[2,64,256]{2,1,0:T(8,128)(2,1)S(1)} %get-tuple-element.13.content, f32[2,64,256]{2,1,0:T(8,128)S(1)} %get-tuple-element.14.gate, ...), custom_call_target="tpu_custom_call" | custom-call | flops 67108864 | bytes 524288 | tf_op jit(solution)/shard_map/attend/pallas_call | solution.py:279
  19.7 0.0 copy-start.1
  19.7 3.5 %all-to-all-start.1 = ((bf16[8,48,128]{2,1,0:T(8,128)(2,1)}), bf16[8,48,128]{2,1,0:T(8,128)(2,1)S(1)}, u32[]{:S(2)}, u32[]{:S(2)}) async-start(bf16[8,48,128]{2,1,0:T(8,128)(2,1)} %get-tuple-element.18), calls=%async_computation.1 | async-start | bytes 196608 | tf_op jit(solution)/shard_map/all_to_all | solution.py:300
  23.2 0.0 copy-start.11
  23.3 0.0 copy-done.3
  23.3 0.0 copy-done.1
  23.3 0.6 %copy-done.11 = s32[64]{0:T(128)S(1)} copy-done((s32[64]{0:T(128)S(1)}, s32[64]{0:T(128)}, u32[]{:S(2)}) %copy-start.11) | copy-done | bytes 280
  23.9 1.1 %prepare.1 = (f32[8,64,128]{2,1,0:T(8,128)S(1)}, f32[8,64,128]{2,1,0:T(8,128)S(1)}, bf16[32,4096]{1,0:T(8,128)(2,1)S(1)}) custom-call(s32[64]{0:T(128)S(1)} %copy-done.8, s32[64]{0:T(128)S(1)} %copy-done.11, s32[1,64]{1,0:T(1,128)S(1)} %bitcast.6, s32[1,64]{1,0:T(1,128)S(1)} %bitcast.8, f32[2,128]{1,0:T(2,128)S(1)} %copy-done.9, ...), custom_call_target="tpu_custom_call" | custom-call | flops 1048576 | bytes 1048576 | tf_op jit(solution)/shard_map/prepare/pallas_call | solution.py:302
  25.0 5.3 %all-to-all-done.1.got = bf16[8,48,128]{2,1,0:T(8,128)(2,1)S(1)} async-done(((bf16[8,48,128]{2,1,0:T(8,128)(2,1)}), bf16[8,48,128]{2,1,0:T(8,128)(2,1)S(1)}, u32[]{:S(2)}, u32[]{:S(2)}) %all-to-all-start.1) | async-done | bytes 98336 | tf_op jit(solution)/shard_map/all_to_all | solution.py:300
  30.3 1.3 %outer_mean.1 = bf16[8,64,128]{2,1,0:T(8,128)(2,1)} custom-call(bf16[8,48,128]{2,1,0:T(8,128)(2,1)S(1)} %all-to-all-done.1.got, bf16[32,4096]{1,0:T(8,128)(2,1)S(1)} %get-tuple-element.19.spread, f32[8,64,128]{2,1,0:T(8,128)S(1)} %get-tuple-element.20.pair, f32[8,64,128]{2,1,0:T(8,128)S(1)} %get-tuple-element.21.scale), custom_call_target="tpu_custom_call" | custom-call | flops 134217728 | bytes 1048576 | tf_op jit(solution)/shard_map/outer_mean/pallas_call | solution.py:325
Async XLA Ops:
  0.6 0.7 %copy-start.10 = (bf16[128,8]{0,1:T(8,128)(2,1)S(1)}, bf16[128,8]{0,1:T(8,128)(2,1)}, u32[]{:S(2)}) copy-start(bf16[128,8]{0,1:T(8,128)(2,1)} %param.19) | copy-start | bytes 6148
  0.6 0.7 %copy-start.8 = (s32[64]{0:T(128)S(1)}, s32[64]{0:T(128)}, u32[]{:S(2)}) copy-start(s32[64]{0:T(128)} %ids.3) | copy-start | bytes 772
  0.7 0.7 %copy-start.9 = (f32[2,128]{1,0:T(2,128)S(1)}, f32[2,128]{1,0:T(2,128)}, u32[]{:S(2)}) copy-start(f32[2,128]{1,0:T(2,128)} %emb.3) | copy-start | bytes 3076
  1.3 0.9 %copy-start = (bf16[8,64,128]{2,1,0:T(8,128)(2,1)S(1)}, bf16[8,64,128]{2,1,0:T(8,128)(2,1)}, u32[]{:S(2)}) copy-start(bf16[8,64,128]{2,1,0:T(8,128)(2,1)} %x.7) | copy-start | bytes 393220
  3.9 7.4 %copy-start.4 = (bf16[2,64,256]{2,1,0:T(8,128)(2,1)S(1)}, bf16[2,64,256]{2,1,0:T(8,128)(2,1)}, u32[]{:S(2)}) copy-start(bf16[2,64,256]{2,1,0:T(8,128)(2,1)} %x.6) | copy-start | bytes 196612
  3.9 7.4 %copy-start.6 = (s32[16,64]{1,0:T(8,128)S(1)}, s32[16,64]{1,0:T(8,128)}, u32[]{:S(2)}) copy-start(s32[16,64]{1,0:T(8,128)} %presence.3) | copy-start | bytes 12292
  3.9 14.3 %all-to-all-start = ((bf16[8,32,128]{2,1,0:T(8,128)(2,1)}), bf16[8,32,128]{2,1,0:T(8,128)(2,1)S(1)}, u32[]{:S(2)}, u32[]{:S(2)}) async-start(bf16[8,32,128]{2,1,0:T(8,128)(2,1)} %pair_bias.1), calls=%async_computation | async-start | bytes 131072 | tf_op jit(solution)/shard_map/all_to_all | solution.py:261
  11.3 1.0 %copy-start.2 = (bf16[256,1024]{1,0:T(8,128)(2,1)S(1)}, bf16[256,1024]{1,0:T(8,128)(2,1)}, u32[]{:S(2)}) copy-start(bf16[256,1024]{1,0:T(8,128)(2,1)} %weights.1) | copy-start | bytes 1572868
  12.4 5.8 %copy-start.5 = (bf16[256,256]{1,0:T(8,128)(2,1)S(1)}, bf16[256,256]{1,0:T(8,128)(2,1)}, u32[]{:S(2)}) copy-start(bf16[256,256]{1,0:T(8,128)(2,1)} %merge.1) | copy-start | bytes 393220
  12.4 5.8 %copy-start.7 = (bf16[256,64]{0,1:T(8,128)(2,1)S(1)}, bf16[256,64]{0,1:T(8,128)(2,1)}, u32[]{:S(2)}) copy-start(bf16[256,64]{0,1:T(8,128)(2,1)} %param.20) | copy-start | bytes 98308
  18.2 5.0 %copy-start.3 = (bf16[1024,128]{1,0:T(8,128)(2,1)S(1)}, bf16[1024,128]{1,0:T(8,128)(2,1)}, u32[]{:S(2)}) copy-start(bf16[1024,128]{1,0:T(8,128)(2,1)} %reduce.1) | copy-start | bytes 786436
  19.7 3.5 %copy-start.1 = (bf16[8,64,128]{2,1,0:T(8,128)(2,1)S(1)}, bf16[8,64,128]{2,1,0:T(8,128)(2,1)}, u32[]{:S(2)}) copy-start(bf16[8,64,128]{2,1,0:T(8,128)(2,1)} %x.7) | copy-start | bytes 393220
  19.7 10.6 %all-to-all-start.1 = ((bf16[8,48,128]{2,1,0:T(8,128)(2,1)}), bf16[8,48,128]{2,1,0:T(8,128)(2,1)S(1)}, u32[]{:S(2)}, u32[]{:S(2)}) async-start(bf16[8,48,128]{2,1,0:T(8,128)(2,1)} %get-tuple-element.18), calls=%async_computation.1 | async-start | bytes 196608 | tf_op jit(solution)/shard_map/all_to_all | solution.py:300
  23.2 0.7 %copy-start.11 = (s32[64]{0:T(128)S(1)}, s32[64]{0:T(128)}, u32[]{:S(2)}) copy-start(s32[64]{0:T(128)} %amino.1) | copy-start | bytes 772

commit v2 on v1

--- a/solution.py
+++ b/solution.py
@@ -12,6 +12,7 @@
 F32 = jnp.float32
 BF16 = jnp.bfloat16
 VMEM_LIMIT = 24 * 1024 * 1024
+VMEM_FULL = 63 * 1024 * 1024
 
 
 def standardize(x):
@@ -36,16 +37,17 @@
 TN = ((0,), (0,))
 
 
-def pair_input(ids, ids_row, emb, x, res_start):
+def pair_input(ids_row, emb, x, chains, res_start):
     rows, size, channels = x.shape
     chain = jnp.broadcast_to(to_column(ids_row[...].astype(F32), size), (size, channels))
+    chains[...] = chain
     other, same = emb[0:1, :], emb[1:2, :]
     for i in range(rows):
-        chain_i = ids[res_start + i].astype(F32)
+        chain_i = chains[pl.ds(res_start + i, 1), :]
         yield x[i].astype(F32) + jnp.where(chain == chain_i, same, other)
 
 
-def bias_kernel(ids, ids_row, emb, x, logit, out):
+def bias_kernel(ids_row, emb, x, logit, out, chains):
     rows, size, _ = x.shape
     heads = logit.shape[0]
     group = heads * rows
@@ -56,7 +58,7 @@
     lane = lax.broadcasted_iota(jnp.int32, (heads, LANES), 1)
     spread = jnp.where((lane % group) // rows == head, 1.0, 0.0).astype(BF16)
     wide = dot(logit[...], spread, TN).astype(BF16)
-    normed = [standardize(z).astype(BF16) for z in pair_input(ids, ids_row, emb, x, res_start)]
+    normed = [standardize(z).astype(BF16) for z in pair_input(ids_row, emb, x, chains, res_start)]
     full = dot(jnp.concatenate(normed, axis=0), wide, NN)
     lane = lax.broadcasted_iota(jnp.int32, (part, LANES), 1)
     total = jnp.zeros((part, LANES), F32)
@@ -99,7 +101,7 @@
     present_row[...] = jnp.concatenate(row_pieces, axis=1)
 
 
-def attend_kernel(bias, scores, content, gate, present, present_row, x, merge, twin, mixed, out):
+def attend_kernel(order, bias, scores, content, gate, present, present_row, x, merge, twin, mixed, out):
     devices, part, _ = bias.shape
     seqs, size, depth = x.shape
     merged = content.shape[2]
@@ -113,7 +115,7 @@
     gated = []
     tables = []
     for block in range(devices // pack):
-        got = [bias[block * pack + n].astype(F32) for n in range(pack)]
+        got = [bias[order.index(block * pack + n)].astype(F32) for n in range(pack)]
         tables.append(
             jnp.concatenate(
                 [
@@ -148,7 +150,7 @@
     for peer in range(devices):
         for block in range(blocks):
             out[peer, block * width : (block + 1) * width, :] = right[:, block * LANES : (block + 1) * LANES]
-    for peer in range(devices):
+    for slot, peer in enumerate(order):
         rows_here = []
         for s in range(seqs):
             begin = peer * rows
@@ -156,40 +158,40 @@
             rows_here.append(here * present[s, begin : begin + rows, : 2 * width])
         piece = jnp.concatenate(rows_here, axis=0)
         piece = jnp.concatenate([piece, jnp.zeros((seqs * rows, LANES - 2 * width), F32)], axis=1)
-        out[peer, blocks * width :, :] = piece.astype(BF16)
-
-
-def prepare_kernel(ids, amino, ids_row, amino_row, emb, x, presence, reduce, pair, scale, spread, wide):
+        out[slot, blocks * width :, :] = piece.astype(BF16)
+
+
+def prepare_kernel(ids_row, amino_row, emb, x, presence, reduce, pair, scale, spread, wide, chains, keeps):
     rows, size, channels = x.shape
     width = spread.shape[0]
     res_start = lax.axis_index("dap") * rows
-    for i, z in enumerate(pair_input(ids, ids_row, emb, x, res_start)):
+    for i, z in enumerate(pair_input(ids_row, emb, x, chains, res_start)):
         pair[i] = z
     here = presence[...].astype(BF16)
     count = dot(here, here, TN)
     lane = lax.broadcasted_iota(jnp.int32, (size, size), 1)
-    kept = to_column(amino_row[...].astype(F32), size)
+    kept = jnp.broadcast_to(to_column(amino_row[...].astype(F32), size), (size, channels))
+    keeps[...] = kept
     for i in range(rows):
         column = jnp.sum(jnp.where(lane == res_start + i, count, 0.0), axis=1, keepdims=True) + 1.0
-        kept_i = amino[res_start + i].astype(F32)
-        scale[i] = jnp.broadcast_to(kept * kept_i / column, (size, channels))
+        scale[i] = kept * keeps[pl.ds(res_start + i, 1), :] / column
     wide[...] = reduce[...].astype(F32)
     for e in range(width):
         spread[:, e * channels : (e + 1) * channels] = wide[pl.ds(e, width, stride=width), :].astype(BF16)
 
 
-def outer_kernel(got, spread, pair, scale, out, right_rows, left_rows):
+def outer_kernel(order, got, spread, pair, scale, out, right_rows, left_rows):
     devices = got.shape[0]
     rows, size, channels = pair.shape
     width = spread.shape[0]
     blocks = right_rows.shape[0]
     seqs = blocks * LANES // size
-    for peer in range(devices):
+    for slot, peer in enumerate(order):
         for block in range(blocks):
             right_rows[block, pl.ds(peer, width, stride=devices), :] = got[
-                peer, block * width : (block + 1) * width, :
+                slot, block * width : (block + 1) * width, :
             ].astype(F32)
-        left_rows[pl.ds(peer, seqs * rows, stride=devices), :] = got[peer, blocks * width :, :].astype(F32)
+        left_rows[pl.ds(peer, seqs * rows, stride=devices), :] = got[slot, blocks * width :, :].astype(F32)
     right = jnp.concatenate([jnp.transpose(right_rows[block]) for block in range(blocks)], axis=0).astype(BF16)
     left = left_rows[...][:, :width].astype(BF16)
     table = dot(left, spread[...], NN)
@@ -204,22 +206,22 @@
         out[i] = (pair[i] + scale[i] * update).astype(BF16)
 
 
+def member_order(devices):
+    return [(5 * devices // 8 - n) % devices for n in range(devices)]
+
+
 def vmem(count):
     return [pl.BlockSpec(memory_space=pltpu.VMEM) for _ in range(count)]
 
 
-def smem(count):
-    return [pl.BlockSpec(memory_space=pltpu.SMEM) for _ in range(count)]
-
-
-def call(body, shapes, in_specs, name, flops, moved, scratch=()):
+def call(body, shapes, in_specs, name, flops, moved, scratch=(), limit=VMEM_LIMIT):
     return pl.pallas_call(
         body,
         out_shape=shapes,
         in_specs=in_specs,
         out_specs=jax.tree.map(lambda _: pl.BlockSpec(memory_space=pltpu.VMEM), shapes),
         scratch_shapes=list(scratch),
-        compiler_params=pltpu.CompilerParams(vmem_limit_bytes=VMEM_LIMIT),
+        compiler_params=pltpu.CompilerParams(vmem_limit_bytes=limit),
         cost_estimate=pl.CostEstimate(flops=flops, bytes_accessed=moved, transcendentals=0),
         name=name,
     )
@@ -247,18 +249,21 @@
     group = heads * rows
     pack = LANES // group
     struct = jax.ShapeDtypeStruct
+    order = member_order(devices)
     ids_row = strand_identity.reshape(1, size)
     amino_row = amino_presence.reshape(1, size)
 
     bias = call(
         bias_kernel,
         struct((devices, size // pack, LANES), BF16),
-        smem(1) + vmem(4),
+        vmem(4),
         "pair_bias",
         2 * rows * size * channels * LANES,
         2 * rows * size * channels,
-    )(strand_identity, ids_row, strand_couple_embedding, couple_features, couple_logit_matrix.T)
-    bias = lax.all_to_all(bias, "dap", 0, 0)
+        [pltpu.VMEM((size, channels), F32)],
+        VMEM_FULL,
+    )(ids_row, strand_couple_embedding, couple_features, couple_logit_matrix.T)
+    bias = lax.all_to_all(bias, "dap", 0, 0, axis_index_groups=[order])
 
     scores, content, gate, present, present_row = call(
         functools.partial(project_kernel, rows),
@@ -277,9 +282,9 @@
 
     blocks = seqs * size // LANES
     mixed, factors = call(
-        attend_kernel,
+        functools.partial(attend_kernel, order),
         (
-            struct(alignment_features.shape, BF16),
+            pltpu.VMEM(alignment_features.shape, BF16),
             struct((devices, blocks * width + seqs * rows, LANES), BF16),
         ),
         vmem(9),
@@ -297,7 +302,7 @@
         heads_merge_matrix,
         twin_factor_matrix.T,
     )
-    factors = lax.all_to_all(factors, "dap", 0, 0)
+    factors = lax.all_to_all(factors, "dap", 0, 0, axis_index_groups=[order])
 
     pair, scale, spread = call(
         prepare_kernel,
@@ -306,14 +311,16 @@
             struct(couple_features.shape, F32),
             struct((width, width * channels), BF16),
         ),
-        smem(2) + vmem(6),
+        vmem(6),
         "prepare",
         16 * rows * size * channels,
         16 * rows * size * channels,
-        [pltpu.VMEM((width * width, channels), F32)],
+        [
+            pltpu.VMEM((width * width, channels), F32),
+            pltpu.VMEM((size, channels), F32),
+            pltpu.VMEM((size, channels), F32),
+        ],
     )(
-        strand_identity,
-        amino_presence,
         ids_row,
         amino_row,
         strand_couple_embedding,
@@ -323,7 +330,7 @@
     )
 
     refreshed = call(
-        outer_kernel,
+        functools.partial(outer_kernel, order),
         struct(couple_features.shape, BF16),
         vmem(4),
         "outer_mean",

time: 32.1 us -> 26.9 us (0.84)
  waiting for transfers between devices: 10.5 us -> 3.31 us
  starting transfers between devices: 10.9 us -> 14.1 us
  local copies, waits for them, and re-layouts: 3.28 us -> 2.35 us
    all_to_all x2, waiting for transfers between devices: 10.5 us -> 3.31 us  [the longest x1 1.74 us: on_device(): bias = lax.all_to_all(bias, 'dap', 0, 0, axis_index_groups=[order])]
    all_to_all x2, starting transfers between devices: 10.9 us -> 14.1 us  [the longest x1 8.4 us: on_device(): bias = lax.all_to_all(bias, 'dap', 0, 0, axis_index_groups=[order])]
    unnamed x24 -> x21, local copies, waits for them, and re-layouts: 3.28 us -> 2.35 us
    pallas_call x1, Pallas kernels: 1.13 us -> 0.59 us  [on_device(): call(prepare_kernel, (struct(couple_features.shape, F32), struct(couple_f...]
    pallas_call x3, Pallas kernels: 4.5 us -> 4.9 us  [the longest x1 2.03 us: on_device(): call(bias_kernel, struct((devices, size // pack, LANES), BF16), vmem(4),...]
  transfers between devices with their start and end apart: 2 -> 2, of which waited for: 2 -> 2; matrix products, arithmetic and copies ran while one was open for 0% -> 2% of each run, Pallas kernels for 6% -> 5%
where the time goes in v2:
time: 26.9 us; the launch traced here: 26.5 us
  starting transfers between devices  14.1 us (52%)
  Pallas kernels  6.09 us (23%)
  waiting for transfers between devices  3.31 us (12%)
  local copies, waits for them, and re-layouts  2.35 us (9%)
  between operations  0.68 us (3%)
    all_to_all x1, starting transfers between devices, on_device(): bias = lax.all_to_all(bias, 'dap', 0, 0, axis_index_groups=[order])  8.4 us
    all_to_all x1, starting transfers between devices, on_device(): factors = lax.all_to_all(factors, 'dap', 0, 0, axis_index_groups=[order])  5.68 us
    unnamed x21, local copies, waits for them, and re-layouts  2.35 us
    pallas_call x1, Pallas kernels, on_device(): call(bias_kernel, struct((devices, size // pack, LANES), BF16), vmem(4),...  2.03 us
    all_to_all x1, waiting for transfers between devices, on_device(): bias = lax.all_to_all(bias, 'dap', 0, 0, axis_index_groups=[order])  1.74 us
    all_to_all x1, waiting for transfers between devices, on_device(): factors = lax.all_to_all(factors, 'dap', 0, 0, axis_index_groups=[order])  1.57 us
    pallas_call x1, Pallas kernels, on_device(): call(functools.partial(attend_kernel, order), (pltpu.VMEM(alignment_featu...  1.53 us
    pallas_call x1, Pallas kernels, on_device(): call(functools.partial(outer_kernel, order), struct(couple_features.shape...  1.34 us
  transfers between devices with their start and end apart: 2, of which 2 were waited for; matrix products, arithmetic and copies ran while one was open for 2% of the time, Pallas kernels for 5%

profile of v2, /device:TPU:0, one launch (start us, length us, event | category | flops | bytes accessed | tf_op | source)
XLA Modules:
  0.0 26.5 jit_solution(11889565566096059415)
XLA Ops:
  0.6 2.0 %pair_bias.1 = bf16[8,32,128]{2,1,0:T(8,128)(2,1)} custom-call(s32[1,64]{1,0:T(1,128)} %bitcast.5, f32[2,128]{1,0:T(2,128)} %emb.3, bf16[8,64,128]{2,1,0:T(8,128)(2,1)} %x.7, bf16[8,128]{1,0:T(8,128)(2,1)} %bitcast.8), custom_call_target="tpu_custom_call" | custom-call | flops 16777216 | bytes 131072 | tf_op jit(solution)/shard_map/pair_bias/pallas_call | solution.py:256
  2.7 0.0 copy-start.3
  2.7 0.0 copy-start.5
  2.7 8.4 %all-to-all-start = ((bf16[8,32,128]{2,1,0:T(8,128)(2,1)}), bf16[8,32,128]{2,1,0:T(8,128)(2,1)S(1)}, u32[]{:S(2)}, u32[]{:S(2)}) async-start(bf16[8,32,128]{2,1,0:T(8,128)(2,1)} %pair_bias.1), calls=%async_computation | async-start | bytes 131072 | tf_op jit(solution)/shard_map/all_to_all | solution.py:266
  11.1 0.0 copy-done.3
  11.1 0.0 copy-done.5
  11.1 0.0 copy-start.1
  11.1 1.0 %copy-done.1 = bf16[256,1024]{1,0:T(8,128)(2,1)S(1)} copy-done((bf16[256,1024]{1,0:T(8,128)(2,1)S(1)}, bf16[256,1024]{1,0:T(8,128)(2,1)}, u32[]{:S(2)}) %copy-start.1) | copy-done | bytes 524312
  12.1 0.0 copy-start.4
  12.1 0.0 copy-start.6
  12.1 0.6 %project.1 = (f32[2,64,512]{2,1,0:T(8,128)S(1)}, bf16[2,64,256]{2,1,0:T(8,128)(2,1)S(1)}, f32[2,64,256]{2,1,0:T(8,128)S(1)}, f32[2,64,128]{2,1,0:T(8,128)S(1)}, f32[1,128]{1,0:T(1,128)S(1)}) custom-call(bf16[2,64,256]{2,1,0:T(8,128)(2,1)S(1)} %copy-done.3, bf16[256,1024]{1,0:T(8,128)(2,1)S(1)} %copy-done.1, s32[16,64]{1,0:T(8,128)S(1)} %copy-done.5), custom_call_target="tpu_custom_call" | custom-call | flops 100663296 | bytes 524288 | tf_op jit(solution)/shard_map/project/pallas_call | solution.py:268
  12.7 1.7 %all-to-all-done.bias = bf16[8,32,128]{2,1,0:T(8,128)(2,1)S(1)} async-done(((bf16[8,32,128]{2,1,0:T(8,128)(2,1)}), bf16[8,32,128]{2,1,0:T(8,128)(2,1)S(1)}, u32[]{:S(2)}, u32[]{:S(2)}) %all-to-all-start) | async-done | bytes 65568 | tf_op jit(solution)/shard_map/all_to_all | solution.py:266
  14.5 0.0 copy-done.4
  14.5 0.0 copy-done.6
  14.5 0.0 copy-start.2
  14.5 1.5 %attend.1 = (bf16[2,64,256]{2,1,0:T(8,128)(2,1)S(1)}, bf16[8,48,128]{2,1,0:T(8,128)(2,1)}) custom-call(bf16[8,32,128]{2,1,0:T(8,128)(2,1)S(1)} %all-to-all-done.bias, f32[2,64,512]{2,1,0:T(8,128)S(1)} %get-tuple-element.12.scores, bf16[2,64,256]{2,1,0:T(8,128)(2,1)S(1)} %get-tuple-element.13.content, f32[2,64,256]{2,1,0:T(8,128)S(1)} %get-tuple-element.14.gate, ...), custom_call_target="tpu_custom_call" | custom-call | flops 67108864 | bytes 524288 | tf_op jit(solution)/shard_map/attend/pallas_call | solution.py:284
  16.0 0.0 copy-start
  16.0 0.0 copy-start.9
  16.0 5.7 %all-to-all-start.1 = ((bf16[8,48,128]{2,1,0:T(8,128)(2,1)}), bf16[8,48,128]{2,1,0:T(8,128)(2,1)S(1)}, u32[]{:S(2)}, u32[]{:S(2)}) async-start(bf16[8,48,128]{2,1,0:T(8,128)(2,1)} %get-tuple-element.18), calls=%async_computation.1 | async-start | bytes 196608 | tf_op jit(solution)/shard_map/all_to_all | solution.py:305
  21.7 0.0 copy-start.7
  21.7 0.0 copy-start.8
  21.7 0.0 copy-done.2
  21.7 0.0 copy-done
  21.7 0.0 copy-done.9
  21.7 0.6 %copy-done.7 = f32[2,128]{1,0:T(2,128)S(1)} copy-done((f32[2,128]{1,0:T(2,128)S(1)}, f32[2,128]{1,0:T(2,128)}, u32[]{:S(2)}) %copy-start.7) | copy-done | bytes 1048
  22.4 0.0 copy-done.8
  22.4 0.6 %prepare.1 = (f32[8,64,128]{2,1,0:T(8,128)S(1)}, f32[8,64,128]{2,1,0:T(8,128)S(1)}, bf16[32,4096]{1,0:T(8,128)(2,1)S(1)}) custom-call(s32[1,64]{1,0:T(1,128)S(1)} %bitcast.6, s32[1,64]{1,0:T(1,128)S(1)} %bitcast.7, f32[2,128]{1,0:T(2,128)S(1)} %copy-done.7, bf16[8,64,128]{2,1,0:T(8,128)(2,1)S(1)} %copy-done, s32[16,64]{1,0:T(8,128)S(1)} %copy-done.5, ...), custom_call_target="tpu_custom_call" | custom-call | flops 1048576 | bytes 1048576 | tf_op jit(solution)/shard_map/prepare/pallas_call | solution.py:307
  23.0 0.6 %copy.13 = bf16[2,64,256]{2,1,0:T(8,128)(2,1)} copy(bf16[2,64,256]{2,1,0:T(8,128)(2,1)S(1)} %get-tuple-element.22) | data formatting | bytes 131072
  23.6 1.6 %all-to-all-done.1.got = bf16[8,48,128]{2,1,0:T(8,128)(2,1)S(1)} async-done(((bf16[8,48,128]{2,1,0:T(8,128)(2,1)}), bf16[8,48,128]{2,1,0:T(8,128)(2,1)S(1)}, u32[]{:S(2)}, u32[]{:S(2)}) %all-to-all-start.1) | async-done | bytes 98336 | tf_op jit(solution)/shard_map/all_to_all | solution.py:305
  25.2 1.3 %outer_mean.1 = bf16[8,64,128]{2,1,0:T(8,128)(2,1)} custom-call(bf16[8,48,128]{2,1,0:T(8,128)(2,1)S(1)} %all-to-all-done.1.got, bf16[32,4096]{1,0:T(8,128)(2,1)S(1)} %get-tuple-element.19.spread, f32[8,64,128]{2,1,0:T(8,128)S(1)} %get-tuple-element.20.pair, f32[8,64,128]{2,1,0:T(8,128)S(1)} %get-tuple-element.21.scale), custom_call_target="tpu_custom_call" | custom-call | flops 134217728 | bytes 1048576 | tf_op jit(solution)/shard_map/outer_mean/pallas_call | solution.py:332
Async XLA Ops:
  2.7 8.4 %copy-start.3 = (bf16[2,64,256]{2,1,0:T(8,128)(2,1)S(1)}, bf16[2,64,256]{2,1,0:T(8,128)(2,1)}, u32[]{:S(2)}) copy-start(bf16[2,64,256]{2,1,0:T(8,128)(2,1)} %x.6) | copy-start | bytes 196612
  2.7 8.4 %copy-start.5 = (s32[16,64]{1,0:T(8,128)S(1)}, s32[16,64]{1,0:T(8,128)}, u32[]{:S(2)}) copy-start(s32[16,64]{1,0:T(8,128)} %presence.3) | copy-start | bytes 12292
  2.7 11.8 %all-to-all-start = ((bf16[8,32,128]{2,1,0:T(8,128)(2,1)}), bf16[8,32,128]{2,1,0:T(8,128)(2,1)S(1)}, u32[]{:S(2)}, u32[]{:S(2)}) async-start(bf16[8,32,128]{2,1,0:T(8,128)(2,1)} %pair_bias.1), calls=%async_computation | async-start | bytes 131072 | tf_op jit(solution)/shard_map/all_to_all | solution.py:266
  11.1 1.0 %copy-start.1 = (bf16[256,1024]{1,0:T(8,128)(2,1)S(1)}, bf16[256,1024]{1,0:T(8,128)(2,1)}, u32[]{:S(2)}) copy-start(bf16[256,1024]{1,0:T(8,128)(2,1)} %weights.1) | copy-start | bytes 1572868
  12.1 2.3 %copy-start.4 = (bf16[256,256]{1,0:T(8,128)(2,1)S(1)}, bf16[256,256]{1,0:T(8,128)(2,1)}, u32[]{:S(2)}) copy-start(bf16[256,256]{1,0:T(8,128)(2,1)} %merge.1) | copy-start | bytes 393220
  12.1 2.3 %copy-start.6 = (bf16[256,64]{0,1:T(8,128)(2,1)S(1)}, bf16[256,64]{0,1:T(8,128)(2,1)}, u32[]{:S(2)}) copy-start(bf16[256,64]{0,1:T(8,128)(2,1)} %param.20) | copy-start | bytes 98308
  14.5 7.2 %copy-start.2 = (bf16[1024,128]{1,0:T(8,128)(2,1)S(1)}, bf16[1024,128]{1,0:T(8,128)(2,1)}, u32[]{:S(2)}) copy-start(bf16[1024,128]{1,0:T(8,128)(2,1)} %reduce.1) | copy-start | bytes 786436
  16.0 5.7 %copy-start = (bf16[8,64,128]{2,1,0:T(8,128)(2,1)S(1)}, bf16[8,64,128]{2,1,0:T(8,128)(2,1)}, u32[]{:S(2)}) copy-start(bf16[8,64,128]{2,1,0:T(8,128)(2,1)} %x.7) | copy-start | bytes 393220
  16.0 5.7 %copy-start.9 = (s32[64]{0:T(128)S(1)}, s32[64]{0:T(128)}, u32[]{:S(2)}) copy-start(s32[64]{0:T(128)} %param.14) | copy-start | bytes 772
  16.0 9.2 %all-to-all-start.1 = ((bf16[8,48,128]{2,1,0:T(8,128)(2,1)}), bf16[8,48,128]{2,1,0:T(8,128)(2,1)S(1)}, u32[]{:S(2)}, u32[]{:S(2)}) async-start(bf16[8,48,128]{2,1,0:T(8,128)(2,1)} %get-tuple-element.18), calls=%async_computation.1 | async-start | bytes 196608 | tf_op jit(solution)/shard_map/all_to_all | solution.py:305
  21.7 0.7 %copy-start.7 = (f32[2,128]{1,0:T(2,128)S(1)}, f32[2,128]{1,0:T(2,128)}, u32[]{:S(2)}) copy-start(f32[2,128]{1,0:T(2,128)} %emb.3) | copy-start | bytes 3076
  21.7 0.7 %copy-start.8 = (s32[64]{0:T(128)S(1)}, s32[64]{0:T(128)}, u32[]{:S(2)}) copy-start(s32[64]{0:T(128)} %param.15) | copy-start | bytes 772

commit v3 on v2

--- a/solution.py
+++ b/solution.py
@@ -72,19 +72,77 @@
         out[peer] = total
 
 
-def project_kernel(rows, x, weights, presence, scores, content, gate, present, present_row):
+def prepare(ids_row, amino_row, emb, x, presence, reduce, pair, scale, spread, wide, chains, keeps):
+    rows, size, channels = x.shape
+    width = spread.shape[0]
+    res_start = lax.axis_index("dap") * rows
+    for i, z in enumerate(pair_input(ids_row, emb, x, chains, res_start)):
+        pair[i] = z
+    here = presence[...].astype(BF16)
+    count = dot(here, here, TN)
+    lane = lax.broadcasted_iota(jnp.int32, (size, size), 1)
+    kept = jnp.broadcast_to(to_column(amino_row[...].astype(F32), size), (size, channels))
+    keeps[...] = kept
+    for i in range(rows):
+        column = jnp.sum(jnp.where(lane == res_start + i, count, 0.0), axis=1, keepdims=True) + 1.0
+        scale[i] = kept * keeps[pl.ds(res_start + i, 1), :] / column
+    wide[...] = reduce[...].astype(F32)
+    for e in range(width):
+        spread[:, e * channels : (e + 1) * channels] = wide[pl.ds(e, width, stride=width), :].astype(BF16)
+
+
+def project_kernel(
+    x_far,
+    weights_far,
+    presence_far,
+    ids_far,
+    amino_far,
+    emb_far,
+    couple_far,
+    reduce_far,
+    scores,
+    content,
+    gate,
+    present,
+    present_row,
+    pair,
+    scale,
+    spread,
+    x,
+    weights,
+    presence,
+    ids_row,
+    amino_row,
+    emb,
+    couple,
+    reduce,
+    wide,
+    chains,
+    keeps,
+    arrived,
+):
+    far = (x_far, weights_far, presence_far, ids_far, amino_far, emb_far, couple_far, reduce_far)
+    near = (x, weights, presence, ids_row, amino_row, emb, couple, reduce)
+    copies = [pltpu.make_async_copy(src, dst, arrived.at[n]) for n, (src, dst) in enumerate(zip(far, near))]
+    for copy in copies:
+        copy.start()
+    copies[0].wait()
     seqs, size, depth = x.shape
+    rows = couple.shape[0]
     merged = content.shape[2]
     group_total = scores.shape[2]
     heads = group_total // size
     head_size = merged // heads
     seq_start = lax.axis_index("dap") * seqs
     normed = standardize(x[...].reshape(seqs * size, depth).astype(F32)).astype(BF16)
+    copies[1].wait()
     mapped = dot(normed, weights[...], NN)
     asking = (mapped[:, :merged] * head_size**-0.5).astype(BF16).astype(F32)
     target = mapped[:, merged : 2 * merged].astype(BF16)
     content[...] = mapped[:, 2 * merged : 3 * merged].astype(BF16).reshape(content.shape)
     gate[...] = jax.nn.sigmoid(mapped[:, 3 * merged :]).reshape(gate.shape)
+    for copy in copies[2:]:
+        copy.wait()
     lane = lax.broadcasted_iota(jnp.int32, (rows, merged), 1)
     row_pieces = []
     for s in range(seqs):
@@ -93,12 +151,13 @@
             here = asking[begin : begin + rows, :]
             for h in range(heads):
                 pieces.append(jnp.where(lane // head_size == h, here, 0.0))
-        spread = jnp.concatenate(pieces, axis=0).astype(BF16)
-        scores[s] = dot(target[s * size : (s + 1) * size, :], spread, NT)
+        masked = jnp.concatenate(pieces, axis=0).astype(BF16)
+        scores[s] = dot(target[s * size : (s + 1) * size, :], masked, NT)
         row = presence[pl.ds(seq_start + s, 1), :].astype(F32)
         present[s] = jnp.broadcast_to(to_column(row, size), (size, LANES))
         row_pieces.append(row)
     present_row[...] = jnp.concatenate(row_pieces, axis=1)
+    prepare(ids_row, amino_row, emb, couple, presence, reduce, pair, scale, spread, wide, chains, keeps)
 
 
 def attend_kernel(order, bias, scores, content, gate, present, present_row, x, merge, twin, mixed, out):
@@ -161,26 +220,9 @@
         out[slot, blocks * width :, :] = piece.astype(BF16)
 
 
-def prepare_kernel(ids_row, amino_row, emb, x, presence, reduce, pair, scale, spread, wide, chains, keeps):
-    rows, size, channels = x.shape
-    width = spread.shape[0]
-    res_start = lax.axis_index("dap") * rows
-    for i, z in enumerate(pair_input(ids_row, emb, x, chains, res_start)):
-        pair[i] = z
-    here = presence[...].astype(BF16)
-    count = dot(here, here, TN)
-    lane = lax.broadcasted_iota(jnp.int32, (size, size), 1)
-    kept = jnp.broadcast_to(to_column(amino_row[...].astype(F32), size), (size, channels))
-    keeps[...] = kept
-    for i in range(rows):
-        column = jnp.sum(jnp.where(lane == res_start + i, count, 0.0), axis=1, keepdims=True) + 1.0
-        scale[i] = kept * keeps[pl.ds(res_start + i, 1), :] / column
-    wide[...] = reduce[...].astype(F32)
-    for e in range(width):
-        spread[:, e * channels : (e + 1) * channels] = wide[pl.ds(e, width, stride=width), :].astype(BF16)
-
-
-def outer_kernel(order, got, spread, pair, scale, out, right_rows, left_rows):
+def outer_kernel(order, got, spread, pair, scale, mixed, out, mixed_out, right_rows, left_rows, done):
+    keep = pltpu.make_async_copy(mixed, mixed_out, done)
+    keep.start()
     devices = got.shape[0]
     rows, size, channels = pair.shape
     width = spread.shape[0]
@@ -204,6 +246,7 @@
             ).astype(BF16)
             update = update + dot(right[s * size : (s + 1) * size, :], columns, NN)
         out[i] = (pair[i] + scale[i] * update).astype(BF16)
+    keep.wait()
 
 
 def member_order(devices):
@@ -265,20 +308,40 @@
     )(ids_row, strand_couple_embedding, couple_features, couple_logit_matrix.T)
     bias = lax.all_to_all(bias, "dap", 0, 0, axis_index_groups=[order])
 
-    scores, content, gate, present, present_row = call(
-        functools.partial(project_kernel, rows),
+    project_inputs = (
+        alignment_features,
+        fourfold_input_matrix,
+        alignment_presence,
+        ids_row,
+        amino_row,
+        strand_couple_embedding,
+        couple_features,
+        tensor_reduce_matrix,
+    )
+    scores, content, gate, present, present_row, pair, scale, spread = call(
+        project_kernel,
         (
             struct((seqs, size, heads * size), F32),
             struct((seqs, size, merged), BF16),
             struct((seqs, size, merged), F32),
             struct((seqs, size, LANES), F32),
             struct((1, seqs * size), F32),
+            struct(couple_features.shape, F32),
+            struct(couple_features.shape, F32),
+            struct((width, width * channels), BF16),
         ),
-        vmem(3),
+        [pl.BlockSpec(memory_space=pltpu.HBM)] * 8,
         "project",
         2 * seqs * size * depth * 4 * merged + 2 * seqs * size * size * heads * merged,
         2 * depth * 4 * merged,
-    )(alignment_features, fourfold_input_matrix, alignment_presence)
+        [pltpu.VMEM(array.shape, array.dtype) for array in project_inputs]
+        + [
+            pltpu.VMEM((width * width, channels), F32),
+            pltpu.VMEM((size, channels), F32),
+            pltpu.VMEM((size, channels), F32),
+            pltpu.SemaphoreType.DMA((len(project_inputs),)),
+        ],
+    )(*[pltpu.with_memory_space_constraint(array, pltpu.HBM) for array in project_inputs])
 
     blocks = seqs * size // LANES
     mixed, factors = call(
@@ -304,43 +367,24 @@
     )
     factors = lax.all_to_all(factors, "dap", 0, 0, axis_index_groups=[order])
 
-    pair, scale, spread = call(
-        prepare_kernel,
-        (
-            struct(couple_features.shape, F32),
-            struct(couple_features.shape, F32),
-            struct((width, width * channels), BF16),
-        ),
-        vmem(6),
-        "prepare",
-        16 * rows * size * channels,
-        16 * rows * size * channels,
-        [
-            pltpu.VMEM((width * width, channels), F32),
-            pltpu.VMEM((size, channels), F32),
-            pltpu.VMEM((size, channels), F32),
-        ],
-    )(
-        ids_row,
-        amino_row,
-        strand_couple_embedding,
-        couple_features,
-        alignment_presence,
-        tensor_reduce_matrix,
-    )
-
-    refreshed = call(
+    refreshed, mixed = pl.pallas_call(
         functools.partial(outer_kernel, order),
-        struct(couple_features.shape, BF16),
-        vmem(4),
-        "outer_mean",
-        4 * rows * size * channels * width * seqs * devices,
-        16 * rows * size * channels,
-        [
+        out_shape=(struct(couple_features.shape, BF16), struct(alignment_features.shape, BF16)),
+        in_specs=vmem(5),
+        out_specs=(pl.BlockSpec(memory_space=pltpu.VMEM), pl.BlockSpec(memory_space=pl.ANY)),
+        scratch_shapes=[
             pltpu.VMEM((blocks, width * devices, LANES), F32),
             pltpu.VMEM((seqs * rows * devices, LANES), F32),
+            pltpu.SemaphoreType.DMA,
         ],
-    )(factors, spread, pair, scale)
+        compiler_params=pltpu.CompilerParams(vmem_limit_bytes=VMEM_LIMIT),
+        cost_estimate=pl.CostEstimate(
+            flops=4 * rows * size * channels * width * seqs * devices,
+            bytes_accessed=16 * rows * size * channels,
+            transcendentals=0,
+        ),
+        name="outer_mean",
+    )(factors, spread, pair, scale, mixed)
     return (mixed, refreshed)
 
 

time: 26.9 us -> 25.5 us (0.948)
  blocking collectives: 0 us -> 8.61 us
  starting transfers between devices: 14.1 us -> 8.27 us
  local copies, waits for them, and re-layouts: 2.35 us -> 0.01 us
  waiting for transfers between devices: 3.31 us -> 1.24 us
  Pallas kernels: 6.09 us -> 6.41 us
    all_to_all x0 -> x1, blocking collectives: none -> 8.61 us  [on_device(): factors = lax.all_to_all(factors, 'dap', 0, 0, axis_index_groups=[order])]
    all_to_all x1 -> x0, starting transfers between devices: 5.68 us -> none  [on_device(): factors = lax.all_to_all(factors, 'dap', 0, 0, axis_index_groups=[order])]
    unnamed x21 -> x6, local copies, waits for them, and re-layouts: 2.35 us -> 0.01 us
    all_to_all x1 -> x0, waiting for transfers between devices: 1.57 us -> none  [on_device(): factors = lax.all_to_all(factors, 'dap', 0, 0, axis_index_groups=[order])]
    pallas_call x3 -> x2, Pallas kernels: 2.53 us -> 3.49 us  [the longest x1 2.14 us: on_device(): call(project_kernel, (struct((seqs, size, heads * size), F32), struct((se...]
    pallas_call x1, Pallas kernels: 1.53 us -> 0.89 us  [on_device(): call(functools.partial(attend_kernel, order), (pltpu.VMEM(alignment_featu...]
    all_to_all x1, waiting for transfers between devices: 1.74 us -> 1.24 us  [on_device(): bias = lax.all_to_all(bias, 'dap', 0, 0, axis_index_groups=[order])]
  transfers between devices with their start and end apart: 2 -> 1, of which waited for: 2 -> 1; matrix products, arithmetic and copies ran while one was open for 2% -> 0% of each run, Pallas kernels for 5% -> 8%
where the time goes in v3:
time: 25.5 us; the launch traced here: 25.2 us
  blocking collectives  8.61 us (34%)
  starting transfers between devices  8.27 us (32%)
  Pallas kernels  6.41 us (25%)
  waiting for transfers between devices  1.24 us (5%)
  between operations  0.66 us (3%)
    all_to_all x1, blocking collectives, on_device(): factors = lax.all_to_all(factors, 'dap', 0, 0, axis_index_groups=[order])  8.61 us
    all_to_all x1, starting transfers between devices, on_device(): bias = lax.all_to_all(bias, 'dap', 0, 0, axis_index_groups=[order])  8.27 us
    pallas_call x1, Pallas kernels, on_device(): call(project_kernel, (struct((seqs, size, heads * size), F32), struct((se...  2.14 us
    pallas_call x1, Pallas kernels, on_device(): call(bias_kernel, struct((devices, size // pack, LANES), BF16), vmem(4),...  2.03 us
    pallas_call x1, Pallas kernels, on_device(): pl.pallas_call(functools.partial(outer_kernel, order), out_shape=(struct(...  1.35 us
    all_to_all x1, waiting for transfers between devices, on_device(): bias = lax.all_to_all(bias, 'dap', 0, 0, axis_index_groups=[order])  1.24 us
    pallas_call x1, Pallas kernels, on_device(): call(functools.partial(attend_kernel, order), (pltpu.VMEM(alignment_featu...  0.89 us
  transfers between devices with their start and end apart: 1, of which 1 were waited for; matrix products, arithmetic and copies ran while one was open for 0% of the time, Pallas kernels for 8%

profile of v3, /device:TPU:0, one launch (start us, length us, event | category | flops | bytes accessed | tf_op | source)
XLA Modules:
  0.0 25.2 jit_solution(4070780605702692112)
XLA Ops:
  0.6 2.0 %pair_bias.1 = bf16[8,32,128]{2,1,0:T(8,128)(2,1)} custom-call(s32[1,64]{1,0:T(1,128)} %bitcast.6, f32[2,128]{1,0:T(2,128)} %emb_far.1, bf16[8,64,128]{2,1,0:T(8,128)(2,1)} %couple_far.1, bf16[8,128]{1,0:T(8,128)(2,1)} %bitcast.5), custom_call_target="tpu_custom_call" | custom-call | flops 16777216 | bytes 131072 | tf_op jit(solution)/shard_map/pair_bias/pallas_call | solution.py:299
  2.7 8.3 %all-to-all-start = ((bf16[8,32,128]{2,1,0:T(8,128)(2,1)}), bf16[8,32,128]{2,1,0:T(8,128)(2,1)S(1)}, u32[]{:S(2)}, u32[]{:S(2)}) async-start(bf16[8,32,128]{2,1,0:T(8,128)(2,1)} %pair_bias.1), calls=%async_computation | async-start | bytes 131072 | tf_op jit(solution)/shard_map/all_to_all | solution.py:309
  10.9 0.0 copy-start
  10.9 0.0 copy-start.1
  10.9 0.0 copy-start.2
  10.9 2.1 %project.1 = (f32[2,64,512]{2,1,0:T(8,128)S(1)}, bf16[2,64,256]{2,1,0:T(8,128)(2,1)S(1)}, f32[2,64,256]{2,1,0:T(8,128)S(1)}, f32[2,64,128]{2,1,0:T(8,128)S(1)}, ...) custom-call(bf16[2,64,256]{2,1,0:T(8,128)(2,1)} %x.3, ...), custom_call_target="tpu_custom_call" | custom-call | flops 100663296 | bytes 524288 | tf_op jit(solution)/shard_map/project/pallas_call | solution.py:321
  13.1 1.2 %all-to-all-done.bias = bf16[8,32,128]{2,1,0:T(8,128)(2,1)S(1)} async-done(((bf16[8,32,128]{2,1,0:T(8,128)(2,1)}), bf16[8,32,128]{2,1,0:T(8,128)(2,1)S(1)}, u32[]{:S(2)}, u32[]{:S(2)}) %all-to-all-start) | async-done | bytes 65568 | tf_op jit(solution)/shard_map/all_to_all | solution.py:309
  14.3 0.0 copy-done
  14.3 0.0 copy-done.1
  14.3 0.0 copy-done.2
  14.3 0.9 %attend.1 = (bf16[2,64,256]{2,1,0:T(8,128)(2,1)S(1)}, bf16[8,48,128]{2,1,0:T(8,128)(2,1)S(1)}) custom-call(bf16[8,32,128]{2,1,0:T(8,128)(2,1)S(1)} %all-to-all-done.bias, f32[2,64,512]{2,1,0:T(8,128)S(1)} %get-tuple-element.14.scores, bf16[2,64,256]{2,1,0:T(8,128)(2,1)S(1)} %get-tuple-element.15.content, f32[2,64,256]{2,1,0:T(8,128)S(1)} %get-tuple-element.16.gate, ...), custom_call_target="tpu_custom_call" | custom-call | flops 67108864 | bytes 524288 | tf_op jit(solution)/shard_map/attend/pallas_call | solution.py:347
  15.2 8.6 %all_to_all.10.got = bf16[8,48,128]{2,1,0:T(8,128)(2,1)S(1)} all-to-all(bf16[8,48,128]{2,1,0:T(8,128)(2,1)S(1)} %get-tuple-element.19), channel_id=1, replica_groups={{5,4,3,2,1,0,7,6},{13,12,11,10,9,8,15,14},{21,20,19,18,17,16,23,22},{29..., dimensions={0} | all-to-all | bytes 196608 | tf_op jit(solution)/shard_map/all_to_all | solution.py:368
  23.8 1.4 %outer_mean.1 = (bf16[8,64,128]{2,1,0:T(8,128)(2,1)}, bf16[2,64,256]{2,1,0:T(8,128)(2,1)}) custom-call(bf16[8,48,128]{2,1,0:T(8,128)(2,1)S(1)} %all_to_all.10.got, bf16[32,4096]{1,0:T(8,128)(2,1)S(1)} %get-tuple-element.20.spread, f32[8,64,128]{2,1,0:T(8,128)S(1)} %get-tuple-element.21.pair, f32[8,64,128]{2,1,0:T(8,128)S(1)} %get-tuple-element.22.scale, ...), custom_call_target="tpu_custom_call" | custom-call | flops 134217728 | bytes 1048576 | tf_op jit(solution)/shard_map/outer_mean/pallas_call | solution.py:370
Async XLA Ops:
  2.7 11.7 %all-to-all-start = ((bf16[8,32,128]{2,1,0:T(8,128)(2,1)}), bf16[8,32,128]{2,1,0:T(8,128)(2,1)S(1)}, u32[]{:S(2)}, u32[]{:S(2)}) async-start(bf16[8,32,128]{2,1,0:T(8,128)(2,1)} %pair_bias.1), calls=%async_computation | async-start | bytes 131072 | tf_op jit(solution)/shard_map/all_to_all | solution.py:309
  10.9 3.4 %copy-start = (bf16[2,64,256]{2,1,0:T(8,128)(2,1)S(1)}, bf16[2,64,256]{2,1,0:T(8,128)(2,1)}, u32[]{:S(2)}) copy-start(bf16[2,64,256]{2,1,0:T(8,128)(2,1)} %x.3) | copy-start | bytes 196612
  10.9 3.4 %copy-start.1 = (bf16[256,256]{1,0:T(8,128)(2,1)S(1)}, bf16[256,256]{1,0:T(8,128)(2,1)}, u32[]{:S(2)}) copy-start(bf16[256,256]{1,0:T(8,128)(2,1)} %merge.1) | copy-start | bytes 393220
  10.9 3.4 %copy-start.2 = (bf16[256,64]{0,1:T(8,128)(2,1)S(1)}, bf16[256,64]{0,1:T(8,128)(2,1)}, u32[]{:S(2)}) copy-start(bf16[256,64]{0,1:T(8,128)(2,1)} %param.20) | copy-start | bytes 98308

commit v4 on v3

--- a/solution.py
+++ b/solution.py
@@ -1,4 +1,5 @@
 import functools
+import math
 
 import jax
 import jax.numpy as jnp
@@ -12,6 +13,8 @@
 F32 = jnp.float32
 BF16 = jnp.bfloat16
 VMEM_LIMIT = 24 * 1024 * 1024
+GROUPS = 8
+PAIR = 2
 VMEM_FULL = 63 * 1024 * 1024
 
 
@@ -74,7 +77,7 @@
 
 def prepare(ids_row, amino_row, emb, x, presence, reduce, pair, scale, spread, wide, chains, keeps):
     rows, size, channels = x.shape
-    width = spread.shape[0]
+    width = spread.shape[0] // GROUPS
     res_start = lax.axis_index("dap") * rows
     for i, z in enumerate(pair_input(ids_row, emb, x, chains, res_start)):
         pair[i] = z
@@ -87,8 +90,12 @@
         column = jnp.sum(jnp.where(lane == res_start + i, count, 0.0), axis=1, keepdims=True) + 1.0
         scale[i] = kept * keeps[pl.ds(res_start + i, 1), :] / column
     wide[...] = reduce[...].astype(F32)
+    each = width // GROUPS
     for e in range(width):
-        spread[:, e * channels : (e + 1) * channels] = wide[pl.ds(e, width, stride=width), :].astype(BF16)
+        group, place = e // each, e % each
+        spread[group * width : (group + 1) * width, place * channels : (place + 1) * channels] = wide[
+            pl.ds(e, width, stride=width), :
+        ].astype(BF16)
 
 
 def project_kernel(
@@ -170,7 +177,7 @@
     heads = group // rows
     head_size = merged // heads
     width = twin.shape[0] // 2
-    lane = lax.broadcasted_iota(jnp.int32, (rows, merged), 1)
+    lane = lax.broadcasted_iota(jnp.int32, (rows, LANES), 1)
     gated = []
     tables = []
     for block in range(devices // pack):
@@ -184,26 +191,38 @@
                 axis=0,
             )
         )
+    tiles = merged // LANES
+    few = heads // tiles
     for s in range(seqs):
         absent = (present[s] - 1.0) * 1000000000.0
-        context = []
+        turned = []
         for block in range(devices // pack):
             logits = scores[s, :, block * LANES : (block + 1) * LANES] + tables[block] + absent
             raised = jnp.exp(logits - jnp.max(logits, axis=0, keepdims=True))
             weights = raised * (1.0 / jnp.sum(raised, axis=0, keepdims=True))
-            mixed_heads = dot(weights.astype(BF16), content[s], TN)
-            for n in range(pack):
-                total = jnp.zeros((rows, merged), F32)
-                for h in range(heads):
-                    begin = n * group + h * rows
-                    total = jnp.where(lane // head_size == h, mixed_heads[begin : begin + rows, :], total)
-                context.append(total)
-        gated.append((gate[s] * jnp.concatenate(context, axis=0)).astype(BF16))
+            turned.append(jnp.transpose(weights.astype(BF16)))
+        context = []
+        for tile in range(tiles):
+            mine = []
+            for block in range(devices // pack):
+                for n in range(pack):
+                    begin = n * group + tile * few * rows
+                    mine.append(turned[block][begin : begin + few * rows, :])
+            product = dot(jnp.concatenate(mine, axis=0), content[s, :, tile * LANES : (tile + 1) * LANES], NN)
+            picked = []
+            for peer in range(devices):
+                total = product[peer * few * rows : peer * few * rows + rows, :]
+                for h in range(1, few):
+                    begin = (peer * few + h) * rows
+                    total = jnp.where(lane // head_size == h, product[begin : begin + rows, :], total)
+                picked.append(total)
+            context.append(jnp.concatenate(picked, axis=0))
+        gated.append((gate[s] * jnp.concatenate(context, axis=1)).astype(BF16))
     offset = dot(jnp.concatenate(gated, axis=0), merge[...], NN)
     updated = (x[...].reshape(seqs * size, depth).astype(F32) + offset).astype(BF16)
     mixed[...] = updated.reshape(mixed.shape)
     normed = standardize(updated.astype(F32)).astype(BF16)
-    left = dot(normed, twin[...], NT)
+    left = dot(normed, jnp.concatenate([twin[:width, :]] * (LANES // width), axis=0), NT)
     right = (dot(twin[width:, :], normed, NT) * present_row[...]).astype(BF16)
     blocks = seqs * size // LANES
     for peer in range(devices):
@@ -214,18 +233,17 @@
         for s in range(seqs):
             begin = peer * rows
             here = left[s * size + begin : s * size + begin + rows, :]
-            rows_here.append(here * present[s, begin : begin + rows, : 2 * width])
-        piece = jnp.concatenate(rows_here, axis=0)
-        piece = jnp.concatenate([piece, jnp.zeros((seqs * rows, LANES - 2 * width), F32)], axis=1)
-        out[slot, blocks * width :, :] = piece.astype(BF16)
-
-
-def outer_kernel(order, got, spread, pair, scale, mixed, out, mixed_out, right_rows, left_rows, done):
-    keep = pltpu.make_async_copy(mixed, mixed_out, done)
-    keep.start()
+            rows_here.append(here * present[s, begin : begin + rows, :])
+        out[slot, blocks * width :, :] = jnp.concatenate(rows_here, axis=0).astype(BF16)
+
+
+def outer_kernel(order, got, spread, pair, scale, mixed, out_far, mixed_out, right_rows, left_rows, out, done):
+    keep = [pltpu.make_async_copy(mixed, mixed_out, done.at[0])]
+    keep[0].start()
     devices = got.shape[0]
     rows, size, channels = pair.shape
-    width = spread.shape[0]
+    width = math.isqrt(spread.shape[0] * spread.shape[1] // channels)
+    groups = spread.shape[0] // width
     blocks = right_rows.shape[0]
     seqs = blocks * LANES // size
     for slot, peer in enumerate(order):
@@ -235,18 +253,39 @@
             ].astype(F32)
         left_rows[pl.ds(peer, seqs * rows, stride=devices), :] = got[slot, blocks * width :, :].astype(F32)
     right = jnp.concatenate([jnp.transpose(right_rows[block]) for block in range(blocks)], axis=0).astype(BF16)
-    left = left_rows[...][:, :width].astype(BF16)
-    table = dot(left, spread[...], NN)
-    for i in range(rows):
-        update = jnp.zeros((size, channels), F32)
+    copies = LANES // width
+    tiles = groups // copies
+    lane = lax.broadcasted_iota(jnp.int32, (seqs * PAIR * devices, LANES), 1)
+    blank = jnp.zeros((seqs * PAIR * devices, LANES), BF16)
+    pieces = []
+    for first in range(0, rows, PAIR):
+        begins = [(s * rows + first + i) * devices for s in range(seqs) for i in range(PAIR)]
+        left = jnp.concatenate([left_rows[begin : begin + devices, :] for begin in begins], axis=0)
+        for group in range(groups):
+            mine = jnp.where(lane // width == group % copies, left, 0.0).astype(BF16)
+            pieces.append(jnp.concatenate([mine if n == group // copies else blank for n in range(tiles)], axis=1))
+    table = dot(jnp.concatenate(pieces, axis=0), spread[...], NN)
+    for first in range(0, rows, PAIR):
+        update = jnp.zeros((size, PAIR * channels), F32)
         for s in range(seqs):
-            begin = (s * rows + i) * devices
-            columns = jnp.concatenate(
-                [table[begin : begin + devices, e * channels : (e + 1) * channels] for e in range(width)], axis=0
-            ).astype(BF16)
+            columns = []
+            for i in range(PAIR):
+                column = []
+                for e in range(width):
+                    group, place = e // (width // groups), e % (width // groups)
+                    begin = ((first // PAIR * groups + group) * seqs * PAIR + s * PAIR + i) * devices
+                    column.append(table[begin : begin + devices, place * channels : (place + 1) * channels])
+                columns.append(jnp.concatenate(column, axis=0).astype(BF16))
+            columns = jnp.concatenate(columns, axis=1)
             update = update + dot(right[s * size : (s + 1) * size, :], columns, NN)
-        out[i] = (pair[i] + scale[i] * update).astype(BF16)
-    keep.wait()
+        for i in range(PAIR):
+            here = update[:, i * channels : (i + 1) * channels]
+            out[first + i] = (pair[first + i] + scale[first + i] * here).astype(BF16)
+        ready = pl.ds(first, PAIR)
+        keep.append(pltpu.make_async_copy(out.at[ready], out_far.at[ready], done.at[1 + first // PAIR]))
+        keep[-1].start()
+    for copy in keep:
+        copy.wait()
 
 
 def member_order(devices):
@@ -328,7 +367,7 @@
             struct((1, seqs * size), F32),
             struct(couple_features.shape, F32),
             struct(couple_features.shape, F32),
-            struct((width, width * channels), BF16),
+            struct((GROUPS * width, width // GROUPS * channels), BF16),
         ),
         [pl.BlockSpec(memory_space=pltpu.HBM)] * 8,
         "project",
@@ -371,11 +410,12 @@
         functools.partial(outer_kernel, order),
         out_shape=(struct(couple_features.shape, BF16), struct(alignment_features.shape, BF16)),
         in_specs=vmem(5),
-        out_specs=(pl.BlockSpec(memory_space=pltpu.VMEM), pl.BlockSpec(memory_space=pl.ANY)),
+        out_specs=(pl.BlockSpec(memory_space=pl.ANY), pl.BlockSpec(memory_space=pl.ANY)),
         scratch_shapes=[
             pltpu.VMEM((blocks, width * devices, LANES), F32),
             pltpu.VMEM((seqs * rows * devices, LANES), F32),
-            pltpu.SemaphoreType.DMA,
+            pltpu.VMEM(couple_features.shape, BF16),
+            pltpu.SemaphoreType.DMA((1 + rows // PAIR,)),
         ],
         compiler_params=pltpu.CompilerParams(vmem_limit_bytes=VMEM_LIMIT),
         cost_estimate=pl.CostEstimate(

time: 25.5 us -> 25.3 us (level)
  transfers between devices with their start and end apart: 1 -> 1, of which waited for: 1 -> 1; matrix products, arithmetic and copies ran while one was open for 0% -> 0% of each run, Pallas kernels for 8% -> 9%
where the time goes in v4:
time: 25.3 us; the launch traced here: 25.1 us
  blocking collectives  8.62 us (34%)
  starting transfers between devices  8.27 us (33%)
  Pallas kernels  6.28 us (25%)
  waiting for transfers between devices  1.24 us (5%)
  between operations  0.66 us (3%)
    all_to_all x1, blocking collectives, on_device(): factors = lax.all_to_all(factors, 'dap', 0, 0, axis_index_groups=[order])  8.62 us
    all_to_all x1, starting transfers between devices, on_device(): bias = lax.all_to_all(bias, 'dap', 0, 0, axis_index_groups=[order])  8.27 us
    pallas_call x1, Pallas kernels, on_device(): call(project_kernel, (struct((seqs, size, heads * size), F32), struct((se...  2.14 us
    pallas_call x1, Pallas kernels, on_device(): call(bias_kernel, struct((devices, size // pack, LANES), BF16), vmem(4),...  2.03 us
    pallas_call x1, Pallas kernels, on_device(): pl.pallas_call(functools.partial(outer_kernel, order), out_shape=(struct(...  1.29 us
    all_to_all x1, waiting for transfers between devices, on_device(): bias = lax.all_to_all(bias, 'dap', 0, 0, axis_index_groups=[order])  1.24 us
    pallas_call x1, Pallas kernels, on_device(): call(functools.partial(attend_kernel, order), (pltpu.VMEM(alignment_featu...  0.82 us
  transfers between devices with their start and end apart: 1, of which 1 were waited for; matrix products, arithmetic and copies ran while one was open for 0% of the time, Pallas kernels for 9%

profile of v4, /device:TPU:0, one launch (start us, length us, event | category | flops | bytes accessed | tf_op | source)
XLA Modules:
  0.0 25.1 jit_solution(3877570355782233808)
XLA Ops:
  0.6 2.0 %pair_bias.1 = bf16[8,32,128]{2,1,0:T(8,128)(2,1)} custom-call(s32[1,64]{1,0:T(1,128)} %bitcast.6, f32[2,128]{1,0:T(2,128)} %emb_far.1, bf16[8,64,128]{2,1,0:T(8,128)(2,1)} %couple_far.1, bf16[8,128]{1,0:T(8,128)(2,1)} %bitcast.5), custom_call_target="tpu_custom_call" | custom-call | flops 16777216 | bytes 131072 | tf_op jit(solution)/shard_map/pair_bias/pallas_call | solution.py:338
  2.7 8.3 %all-to-all-start = ((bf16[8,32,128]{2,1,0:T(8,128)(2,1)}), bf16[8,32,128]{2,1,0:T(8,128)(2,1)S(1)}, u32[]{:S(2)}, u32[]{:S(2)}) async-start(bf16[8,32,128]{2,1,0:T(8,128)(2,1)} %pair_bias.1), calls=%async_computation | async-start | bytes 131072 | tf_op jit(solution)/shard_map/all_to_all | solution.py:348
  10.9 0.0 copy-start
  10.9 0.0 copy-start.1
  10.9 0.0 copy-start.2
  10.9 2.1 %project.1 = (f32[2,64,512]{2,1,0:T(8,128)S(1)}, bf16[2,64,256]{2,1,0:T(8,128)(2,1)S(1)}, f32[2,64,256]{2,1,0:T(8,128)S(1)}, f32[2,64,128]{2,1,0:T(8,128)S(1)}, ...) custom-call(bf16[2,64,256]{2,1,0:T(8,128)(2,1)} %x.3, ...), custom_call_target="tpu_custom_call" | custom-call | flops 100663296 | bytes 524288 | tf_op jit(solution)/shard_map/project/pallas_call | solution.py:360
  13.1 1.2 %all-to-all-done.bias = bf16[8,32,128]{2,1,0:T(8,128)(2,1)S(1)} async-done(((bf16[8,32,128]{2,1,0:T(8,128)(2,1)}), bf16[8,32,128]{2,1,0:T(8,128)(2,1)S(1)}, u32[]{:S(2)}, u32[]{:S(2)}) %all-to-all-start) | async-done | bytes 65568 | tf_op jit(solution)/shard_map/all_to_all | solution.py:348
  14.3 0.0 copy-done
  14.3 0.0 copy-done.1
  14.3 0.0 copy-done.2
  14.3 0.8 %attend.1 = (bf16[2,64,256]{2,1,0:T(8,128)(2,1)S(1)}, bf16[8,48,128]{2,1,0:T(8,128)(2,1)S(1)}) custom-call(bf16[8,32,128]{2,1,0:T(8,128)(2,1)S(1)} %all-to-all-done.bias, f32[2,64,512]{2,1,0:T(8,128)S(1)} %get-tuple-element.14.scores, bf16[2,64,256]{2,1,0:T(8,128)(2,1)S(1)} %get-tuple-element.15.content, f32[2,64,256]{2,1,0:T(8,128)S(1)} %get-tuple-element.16.gate, ...), custom_call_target="tpu_custom_call" | custom-call | flops 67108864 | bytes 524288 | tf_op jit(solution)/shard_map/attend/pallas_call | solution.py:386
  15.2 8.6 %all_to_all.10.got = bf16[8,48,128]{2,1,0:T(8,128)(2,1)S(1)} all-to-all(bf16[8,48,128]{2,1,0:T(8,128)(2,1)S(1)} %get-tuple-element.19), channel_id=1, replica_groups={{5,4,3,2,1,0,7,6},{13,12,11,10,9,8,15,14},{21,20,19,18,17,16,23,22},{29..., dimensions={0} | all-to-all | bytes 196608 | tf_op jit(solution)/shard_map/all_to_all | solution.py:407
  23.8 1.3 %outer_mean.1 = (bf16[8,64,128]{2,1,0:T(8,128)(2,1)}, bf16[2,64,256]{2,1,0:T(8,128)(2,1)}) custom-call(bf16[8,48,128]{2,1,0:T(8,128)(2,1)S(1)} %all_to_all.10.got, bf16[256,512]{1,0:T(8,128)(2,1)S(1)} %get-tuple-element.20.spread, f32[8,64,128]{2,1,0:T(8,128)S(1)} %get-tuple-element.21.pair, f32[8,64,128]{2,1,0:T(8,128)S(1)} %get-tuple-element.22.scale, ...), custom_call_target="tpu_custom_call" | custom-call | flops 134217728 | bytes 1048576 | tf_op jit(solution)/shard_map/outer_mean/pallas_call | solution.py:409
Async XLA Ops:
  2.7 11.7 %all-to-all-start = ((bf16[8,32,128]{2,1,0:T(8,128)(2,1)}), bf16[8,32,128]{2,1,0:T(8,128)(2,1)S(1)}, u32[]{:S(2)}, u32[]{:S(2)}) async-start(bf16[8,32,128]{2,1,0:T(8,128)(2,1)} %pair_bias.1), calls=%async_computation | async-start | bytes 131072 | tf_op jit(solution)/shard_map/all_to_all | solution.py:348
  10.9 3.4 %copy-start = (bf16[2,64,256]{2,1,0:T(8,128)(2,1)S(1)}, bf16[2,64,256]{2,1,0:T(8,128)(2,1)}, u32[]{:S(2)}) copy-start(bf16[2,64,256]{2,1,0:T(8,128)(2,1)} %x.3) | copy-start | bytes 196612
  10.9 3.4 %copy-start.1 = (bf16[256,256]{1,0:T(8,128)(2,1)S(1)}, bf16[256,256]{1,0:T(8,128)(2,1)}, u32[]{:S(2)}) copy-start(bf16[256,256]{1,0:T(8,128)(2,1)} %merge.1) | copy-start | bytes 393220
  10.9 3.4 %copy-start.2 = (bf16[256,64]{0,1:T(8,128)(2,1)S(1)}, bf16[256,64]{0,1:T(8,128)(2,1)}, u32[]{:S(2)}) copy-start(bf16[256,64]{0,1:T(8,128)(2,1)} %param.20) | copy-start | bytes 98308

commit v5 on v4

--- a/solution.py
+++ b/solution.py
@@ -50,19 +50,32 @@
         yield x[i].astype(F32) + jnp.where(chain == chain_i, same, other)
 
 
-def bias_kernel(ids_row, emb, x, logit, out, chains):
+def bias_kernel(*refs):
+    count = (len(refs) - 3) // 2
+    far, out, near = refs[:count], refs[count], refs[count + 1 : 2 * count]
+    logit, chains, arrived = refs[-3:]
+    x, ids_row, emb = near[:3]
+    near = (x, logit, ids_row, emb) + near[3:]
     rows, size, _ = x.shape
+    each = max(1, rows // 4)
+    moves = [(far[0].at[pl.ds(b, each)], x.at[pl.ds(b, each)]) for b in range(0, rows, each)]
+    first = len(moves) + 3
+    moves += list(zip(far[1:], near[1:]))
+    copies = [pltpu.make_async_copy(src, dst, arrived.at[n]) for n, (src, dst) in enumerate(moves)]
+    for copy in copies:
+        copy.start()
+    for copy in copies[:first]:
+        copy.wait()
     heads = logit.shape[0]
     group = heads * rows
     pack = LANES // group
     part = size // pack
     res_start = lax.axis_index("dap") * rows
-    head = lax.broadcasted_iota(jnp.int32, (heads, LANES), 0)
-    lane = lax.broadcasted_iota(jnp.int32, (heads, LANES), 1)
-    spread = jnp.where((lane % group) // rows == head, 1.0, 0.0).astype(BF16)
-    wide = dot(logit[...], spread, TN).astype(BF16)
+    table = logit[...].astype(F32)
+    wide = [jnp.broadcast_to(table[h : h + 1, :], (rows, table.shape[1])) for h in range(heads)] * pack
+    wide = jnp.concatenate(wide, axis=0).astype(BF16)
     normed = [standardize(z).astype(BF16) for z in pair_input(ids_row, emb, x, chains, res_start)]
-    full = dot(jnp.concatenate(normed, axis=0), wide, NN)
+    full = dot(jnp.concatenate(normed, axis=0), wide, NT)
     lane = lax.broadcasted_iota(jnp.int32, (part, LANES), 1)
     total = jnp.zeros((part, LANES), F32)
     for i in range(rows):
@@ -73,6 +86,8 @@
     total = total.astype(BF16)
     for peer in range(out.shape[0]):
         out[peer] = total
+    for copy in copies[first:]:
+        copy.wait()
 
 
 def prepare(ids_row, amino_row, emb, x, presence, reduce, pair, scale, spread, wide, chains, keeps):
@@ -98,15 +113,15 @@
         ].astype(BF16)
 
 
-def project_kernel(
-    x_far,
-    weights_far,
-    presence_far,
-    ids_far,
-    amino_far,
-    emb_far,
-    couple_far,
-    reduce_far,
+def project(
+    x,
+    weights,
+    presence,
+    ids_row,
+    amino_row,
+    emb,
+    couple,
+    reduce,
     scores,
     content,
     gate,
@@ -115,25 +130,10 @@
     pair,
     scale,
     spread,
-    x,
-    weights,
-    presence,
-    ids_row,
-    amino_row,
-    emb,
-    couple,
-    reduce,
     wide,
     chains,
     keeps,
-    arrived,
 ):
-    far = (x_far, weights_far, presence_far, ids_far, amino_far, emb_far, couple_far, reduce_far)
-    near = (x, weights, presence, ids_row, amino_row, emb, couple, reduce)
-    copies = [pltpu.make_async_copy(src, dst, arrived.at[n]) for n, (src, dst) in enumerate(zip(far, near))]
-    for copy in copies:
-        copy.start()
-    copies[0].wait()
     seqs, size, depth = x.shape
     rows = couple.shape[0]
     merged = content.shape[2]
@@ -142,14 +142,11 @@
     head_size = merged // heads
     seq_start = lax.axis_index("dap") * seqs
     normed = standardize(x[...].reshape(seqs * size, depth).astype(F32)).astype(BF16)
-    copies[1].wait()
     mapped = dot(normed, weights[...], NN)
     asking = (mapped[:, :merged] * head_size**-0.5).astype(BF16).astype(F32)
     target = mapped[:, merged : 2 * merged].astype(BF16)
     content[...] = mapped[:, 2 * merged : 3 * merged].astype(BF16).reshape(content.shape)
     gate[...] = jax.nn.sigmoid(mapped[:, 3 * merged :]).reshape(gate.shape)
-    for copy in copies[2:]:
-        copy.wait()
     lane = lax.broadcasted_iota(jnp.int32, (rows, merged), 1)
     row_pieces = []
     for s in range(seqs):
@@ -167,7 +164,7 @@
     prepare(ids_row, amino_row, emb, couple, presence, reduce, pair, scale, spread, wide, chains, keeps)
 
 
-def attend_kernel(order, bias, scores, content, gate, present, present_row, x, merge, twin, mixed, out):
+def attend(order, bias, scores, content, gate, present, present_row, x, merge, twin, mixed, out):
     devices, part, _ = bias.shape
     seqs, size, depth = x.shape
     merged = content.shape[2]
@@ -237,6 +234,40 @@
         out[slot, blocks * width :, :] = jnp.concatenate(rows_here, axis=0).astype(BF16)
 
 
+def middle_kernel(
+    order,
+    bias,
+    x,
+    weights,
+    presence,
+    ids_row,
+    amino_row,
+    emb,
+    couple,
+    reduce,
+    merge,
+    twin,
+    mixed,
+    out,
+    pair,
+    scale,
+    spread,
+    scores,
+    content,
+    gate,
+    present,
+    present_row,
+    wide,
+    chains,
+    keeps,
+):
+    kept = (scores, content, gate, present, present_row)
+    project(
+        x, weights, presence, ids_row, amino_row, emb, couple, reduce, *kept, pair, scale, spread, wide, chains, keeps
+    )
+    attend(order, bias, *kept, x, merge, twin, mixed, out)
+
+
 def outer_kernel(order, got, spread, pair, scale, mixed, out_far, mixed_out, right_rows, left_rows, out, done):
     keep = [pltpu.make_async_copy(mixed, mixed_out, done.at[0])]
     keep[0].start()
@@ -335,75 +366,60 @@
     ids_row = strand_identity.reshape(1, size)
     amino_row = amino_presence.reshape(1, size)
 
-    bias = call(
+    arguments = (
+        couple_features,
+        couple_logit_matrix.T,
+        ids_row,
+        strand_couple_embedding,
+        alignment_features,
+        fourfold_input_matrix,
+        alignment_presence,
+        amino_row,
+        tensor_reduce_matrix,
+        heads_merge_matrix,
+        twin_factor_matrix.T,
+    )
+    bias, couple, ids_row, emb, x, weights, presence, amino_row, reduce, merge, twin = call(
         bias_kernel,
-        struct((devices, size // pack, LANES), BF16),
-        vmem(4),
+        (struct((devices, size // pack, LANES), BF16),)
+        + tuple(pltpu.VMEM(array.shape, array.dtype) for array in arguments[:1] + arguments[2:]),
+        [pl.BlockSpec(memory_space=pltpu.HBM)] * len(arguments),
         "pair_bias",
         2 * rows * size * channels * LANES,
         2 * rows * size * channels,
-        [pltpu.VMEM((size, channels), F32)],
-        VMEM_FULL,
-    )(ids_row, strand_couple_embedding, couple_features, couple_logit_matrix.T)
+        [
+            pltpu.VMEM(arguments[1].shape, BF16),
+            pltpu.VMEM((size, channels), F32),
+            pltpu.SemaphoreType.DMA((len(arguments) + rows,)),
+        ],
+    )(*[pltpu.with_memory_space_constraint(array, pltpu.HBM) for array in arguments])
     bias = lax.all_to_all(bias, "dap", 0, 0, axis_index_groups=[order])
 
-    project_inputs = (
-        alignment_features,
-        fourfold_input_matrix,
-        alignment_presence,
-        ids_row,
-        amino_row,
-        strand_couple_embedding,
-        couple_features,
-        tensor_reduce_matrix,
-    )
-    scores, content, gate, present, present_row, pair, scale, spread = call(
-        project_kernel,
+    blocks = seqs * size // LANES
+    mixed, factors, pair, scale, spread = call(
+        functools.partial(middle_kernel, order),
         (
-            struct((seqs, size, heads * size), F32),
-            struct((seqs, size, merged), BF16),
-            struct((seqs, size, merged), F32),
-            struct((seqs, size, LANES), F32),
-            struct((1, seqs * size), F32),
+            pltpu.VMEM(alignment_features.shape, BF16),
+            struct((devices, blocks * width + seqs * rows, LANES), BF16),
             struct(couple_features.shape, F32),
             struct(couple_features.shape, F32),
             struct((GROUPS * width, width // GROUPS * channels), BF16),
         ),
-        [pl.BlockSpec(memory_space=pltpu.HBM)] * 8,
-        "project",
-        2 * seqs * size * depth * 4 * merged + 2 * seqs * size * size * heads * merged,
-        2 * depth * 4 * merged,
-        [pltpu.VMEM(array.shape, array.dtype) for array in project_inputs]
-        + [
+        vmem(11),
+        "attend",
+        2 * seqs * size * depth * 4 * merged + 6 * seqs * size * size * heads * merged,
+        2 * depth * 4 * merged + 8 * seqs * size * size * heads,
+        [
+            pltpu.VMEM((seqs, size, heads * size), F32),
+            pltpu.VMEM((seqs, size, merged), BF16),
+            pltpu.VMEM((seqs, size, merged), F32),
+            pltpu.VMEM((seqs, size, LANES), F32),
+            pltpu.VMEM((1, seqs * size), F32),
             pltpu.VMEM((width * width, channels), F32),
             pltpu.VMEM((size, channels), F32),
             pltpu.VMEM((size, channels), F32),
-            pltpu.SemaphoreType.DMA((len(project_inputs),)),
         ],
-    )(*[pltpu.with_memory_space_constraint(array, pltpu.HBM) for array in project_inputs])
-
-    blocks = seqs * size // LANES
-    mixed, factors = call(
-        functools.partial(attend_kernel, order),
-        (
-            pltpu.VMEM(alignment_features.shape, BF16),
-            struct((devices, blocks * width + seqs * rows, LANES), BF16),
-        ),
-        vmem(9),
-        "attend",
-        4 * seqs * size * size * heads * merged,
-        8 * seqs * size * size * heads,
-    )(
-        bias,
-        scores,
-        content,
-        gate,
-        present,
-        present_row,
-        alignment_features,
-        heads_merge_matrix,
-        twin_factor_matrix.T,
-    )
+    )(bias, x, weights, presence, ids_row, amino_row, emb, couple, reduce, merge, twin)
     factors = lax.all_to_all(factors, "dap", 0, 0, axis_index_groups=[order])
 
     refreshed, mixed = pl.pallas_call(

time: 25.3 us -> 24.9 us (0.984)
  blocking collectives: 8.62 us -> 19.6 us
  starting transfers between devices: 8.27 us -> 0 us
  Pallas kernels: 6.28 us -> 4.34 us
  waiting for transfers between devices: 1.24 us -> 0 us
    all_to_all x0 -> x1, blocking collectives: none -> 11 us  [on_device(): bias = lax.all_to_all(bias, 'dap', 0, 0, axis_index_groups=[order])]
    all_to_all x1 -> x0, starting transfers between devices: 8.27 us -> none  [on_device(): bias = lax.all_to_all(bias, 'dap', 0, 0, axis_index_groups=[order])]
    pallas_call x3 -> x2, Pallas kernels: 4.99 us -> 3.06 us  [the longest x1 1.57 us: on_device(): call(functools.partial(middle_kernel, order), (pltpu.VMEM(alignment_featu...]
    all_to_all x1 -> x0, waiting for transfers between devices: 1.24 us -> none  [on_device(): bias = lax.all_to_all(bias, 'dap', 0, 0, axis_index_groups=[order])]
  transfers between devices with their start and end apart: 1 -> 0, of which waited for: 1 -> 0; matrix products, arithmetic and copies ran while one was open for 0% -> 0% of each run, Pallas kernels for 9% -> 0%
where the time goes in v5:
time: 24.9 us; the launch traced here: 24.6 us
  blocking collectives  19.6 us (79%)
  Pallas kernels  4.34 us (17%)
  between operations  0.65 us (3%)
    all_to_all x1, blocking collectives, on_device(): bias = lax.all_to_all(bias, 'dap', 0, 0, axis_index_groups=[order])  11 us
    all_to_all x1, blocking collectives, on_device(): factors = lax.all_to_all(factors, 'dap', 0, 0, axis_index_groups=[order])  8.63 us
    pallas_call x1, Pallas kernels, on_device(): call(functools.partial(middle_kernel, order), (pltpu.VMEM(alignment_featu...  1.57 us
    pallas_call x1, Pallas kernels, on_device(): call(bias_kernel, (struct((devices, size // pack, LANES), BF16),) + tuple...  1.49 us
    pallas_call x1, Pallas kernels, on_device(): pl.pallas_call(functools.partial(outer_kernel, order), out_shape=(struct(...  1.28 us

profile of v5, /device:TPU:0, one launch (start us, length us, event | category | flops | bytes accessed | tf_op | source)
XLA Modules:
  0.0 24.6 jit_solution(11843167679434202146)
XLA Ops:
  0.6 1.5 %pair_bias.1 = (bf16[8,32,128]{2,1,0:T(8,128)(2,1)S(1)}, bf16[8,64,128]{2,1,0:T(8,128)(2,1)S(1)}, s32[1,64]{1,0:T(1,128)S(1)}, f32[2,128]{1,0:T(2,128)S(1)}, bf1...) custom-call(bf16[8,64,128]{2,1,0:T(8,128)(2,1)} %refs_0_.1, ...), custom_call_target="tpu_custom_call" | custom-call | flops 16777216 | bytes 131072 | tf_op jit(solution)/shard_map/pair_bias/pallas_call | solution.py:382
  2.1 11.0 %all_to_all.10.bias = bf16[8,32,128]{2,1,0:T(8,128)(2,1)S(1)} all-to-all(bf16[8,32,128]{2,1,0:T(8,128)(2,1)S(1)} %get-tuple-element.20), channel_id=1, replica_groups={{5,4,3,2,1,0,7,6},{13,12,11,10,9,8,15,14},{21,20,19,18,17,16,23,22},{29..., dimensions={0} | all-to-all | bytes 131072 | tf_op jit(solution)/shard_map/all_to_all | solution.py:396
  13.2 1.6 %attend.1 = (bf16[2,64,256]{2,1,0:T(8,128)(2,1)S(1)}, bf16[8,48,128]{2,1,0:T(8,128)(2,1)S(1)}, f32[8,64,128]{2,1,0:T(8,128)S(1)}, f32[8,64,128]{2,1,0:T(8,128)S(1)}, bf16[256,512]{1,0:T(8,128)(2,1)S(1)}) custom-call(bf16[8,32,128]{2,1,0:T(8,128)(2,1)S(1)} %all_to_all.10.bias, bf16[2,64,256]{2,1,0:T(8,128)(2,1)S(1)} %get-tuple-element.21.x, ...), custom_call_target="tpu_custom_call" | custom-call | flops 167772160 | bytes 1048576 | tf_op jit(solution)/shard_map/attend/pallas_call | solution.py:399
  14.7 8.6 %all_to_all.11.got = bf16[8,48,128]{2,1,0:T(8,128)(2,1)S(1)} all-to-all(bf16[8,48,128]{2,1,0:T(8,128)(2,1)S(1)} %get-tuple-element.31), channel_id=1, replica_groups={{5,4,3,2,1,0,7,6},{13,12,11,10,9,8,15,14},{21,20,19,18,17,16,23,22},{29..., dimensions={0} | all-to-all | bytes 196608 | tf_op jit(solution)/shard_map/all_to_all | solution.py:423
  23.4 1.3 %outer_mean.1 = (bf16[8,64,128]{2,1,0:T(8,128)(2,1)}, bf16[2,64,256]{2,1,0:T(8,128)(2,1)}) custom-call(bf16[8,48,128]{2,1,0:T(8,128)(2,1)S(1)} %all_to_all.11.got, bf16[256,512]{1,0:T(8,128)(2,1)S(1)} %get-tuple-element.32.spread, f32[8,64,128]{2,1,0:T(8,128)S(1)} %get-tuple-element.33.pair, f32[8,64,128]{2,1,0:T(8,128)S(1)} %get-tuple-element.34.scale, ...), custom_call_target="tpu_custom_call" | custom-call | flops 134217728 | bytes 1048576 | tf_op jit(solution)/shard_map/outer_mean/pallas_call | solution.py:425

commit v6 on v5

--- a/solution.py
+++ b/solution.py
@@ -104,12 +104,12 @@
     for i in range(rows):
         column = jnp.sum(jnp.where(lane == res_start + i, count, 0.0), axis=1, keepdims=True) + 1.0
         scale[i] = kept * keeps[pl.ds(res_start + i, 1), :] / column
-    wide[...] = reduce[...].astype(F32)
+    turned = jnp.swapaxes(reduce[...].reshape(width, width, channels), 0, 1)
     each = width // GROUPS
     for e in range(width):
         group, place = e // each, e % each
-        spread[group * width : (group + 1) * width, place * channels : (place + 1) * channels] = wide[
-            pl.ds(e, width, stride=width), :
+        spread[group * width : (group + 1) * width, place * channels : (place + 1) * channels] = turned[
+            e
         ].astype(BF16)
 
 

time: 24.9 us -> 24.6 us (0.988)
  no operation moved by 1% of the time
where the time goes in v6:
time: 24.6 us; the launch traced here: 24.4 us
  blocking collectives  19.6 us (80%)
  Pallas kernels  4.11 us (17%)
  between operations  0.65 us (3%)
    all_to_all x1, blocking collectives, on_device(): bias = lax.all_to_all(bias, 'dap', 0, 0, axis_index_groups=[order])  11 us
    all_to_all x1, blocking collectives, on_device(): factors = lax.all_to_all(factors, 'dap', 0, 0, axis_index_groups=[order])  8.63 us
    pallas_call x1, Pallas kernels, on_device(): call(bias_kernel, (struct((devices, size // pack, LANES), BF16),) + tuple...  1.49 us
    pallas_call x1, Pallas kernels, on_device(): call(functools.partial(middle_kernel, order), (pltpu.VMEM(alignment_featu...  1.34 us
    pallas_call x1, Pallas kernels, on_device(): pl.pallas_call(functools.partial(outer_kernel, order), out_shape=(struct(...  1.28 us

profile of v6, /device:TPU:0, one launch (start us, length us, event | category | flops | bytes accessed | tf_op | source)
XLA Modules:
  0.0 24.4 jit_solution(9531920402092644874)
XLA Ops:
  0.6 1.5 %pair_bias.1 = (bf16[8,32,128]{2,1,0:T(8,128)(2,1)S(1)}, bf16[8,64,128]{2,1,0:T(8,128)(2,1)S(1)}, s32[1,64]{1,0:T(1,128)S(1)}, f32[2,128]{1,0:T(2,128)S(1)}, bf1...) custom-call(bf16[8,64,128]{2,1,0:T(8,128)(2,1)} %refs_0_.1, ...), custom_call_target="tpu_custom_call" | custom-call | flops 16777216 | bytes 131072 | tf_op jit(solution)/shard_map/pair_bias/pallas_call | solution.py:382
  2.1 11.0 %all_to_all.10.bias = bf16[8,32,128]{2,1,0:T(8,128)(2,1)S(1)} all-to-all(bf16[8,32,128]{2,1,0:T(8,128)(2,1)S(1)} %get-tuple-element.20), channel_id=1, replica_groups={{5,4,3,2,1,0,7,6},{13,12,11,10,9,8,15,14},{21,20,19,18,17,16,23,22},{29..., dimensions={0} | all-to-all | bytes 131072 | tf_op jit(solution)/shard_map/all_to_all | solution.py:396
  13.2 1.3 %attend.1 = (bf16[2,64,256]{2,1,0:T(8,128)(2,1)S(1)}, bf16[8,48,128]{2,1,0:T(8,128)(2,1)S(1)}, f32[8,64,128]{2,1,0:T(8,128)S(1)}, f32[8,64,128]{2,1,0:T(8,128)S(1)}, bf16[256,512]{1,0:T(8,128)(2,1)S(1)}) custom-call(bf16[8,32,128]{2,1,0:T(8,128)(2,1)S(1)} %all_to_all.10.bias, bf16[2,64,256]{2,1,0:T(8,128)(2,1)S(1)} %get-tuple-element.21.x, ...), custom_call_target="tpu_custom_call" | custom-call | flops 167772160 | bytes 1048576 | tf_op jit(solution)/shard_map/attend/pallas_call | solution.py:399
  14.5 8.6 %all_to_all.11.got = bf16[8,48,128]{2,1,0:T(8,128)(2,1)S(1)} all-to-all(bf16[8,48,128]{2,1,0:T(8,128)(2,1)S(1)} %get-tuple-element.31), channel_id=1, replica_groups={{5,4,3,2,1,0,7,6},{13,12,11,10,9,8,15,14},{21,20,19,18,17,16,23,22},{29..., dimensions={0} | all-to-all | bytes 196608 | tf_op jit(solution)/shard_map/all_to_all | solution.py:423
  23.1 1.3 %outer_mean.1 = (bf16[8,64,128]{2,1,0:T(8,128)(2,1)}, bf16[2,64,256]{2,1,0:T(8,128)(2,1)}) custom-call(bf16[8,48,128]{2,1,0:T(8,128)(2,1)S(1)} %all_to_all.11.got, bf16[256,512]{1,0:T(8,128)(2,1)S(1)} %get-tuple-element.32.spread, f32[8,64,128]{2,1,0:T(8,128)S(1)} %get-tuple-element.33.pair, f32[8,64,128]{2,1,0:T(8,128)S(1)} %get-tuple-element.34.scale, ...), custom_call_target="tpu_custom_call" | custom-call | flops 134217728 | bytes 1048576 | tf_op jit(solution)/shard_map/outer_mean/pallas_call | solution.py:425

commit v7 on v6

--- a/solution.py
+++ b/solution.py
@@ -90,7 +90,7 @@
         copy.wait()
 
 
-def prepare(ids_row, amino_row, emb, x, presence, reduce, pair, scale, spread, wide, chains, keeps):
+def prepare(ids_row, amino_row, emb, x, presence, reduce, pair, scale, spread, chains):
     rows, size, channels = x.shape
     width = spread.shape[0] // GROUPS
     res_start = lax.axis_index("dap") * rows
@@ -99,11 +99,11 @@
     here = presence[...].astype(BF16)
     count = dot(here, here, TN)
     lane = lax.broadcasted_iota(jnp.int32, (size, size), 1)
-    kept = jnp.broadcast_to(to_column(amino_row[...].astype(F32), size), (size, channels))
-    keeps[...] = kept
+    kept = amino_row[...].astype(F32)
+    ratio = to_column(kept, size) * kept / (count + 1.0)
     for i in range(rows):
-        column = jnp.sum(jnp.where(lane == res_start + i, count, 0.0), axis=1, keepdims=True) + 1.0
-        scale[i] = kept * keeps[pl.ds(res_start + i, 1), :] / column
+        column = jnp.sum(jnp.where(lane == res_start + i, ratio, 0.0), axis=1, keepdims=True)
+        scale[i] = jnp.broadcast_to(column, (size, channels))
     turned = jnp.swapaxes(reduce[...].reshape(width, width, channels), 0, 1)
     each = width // GROUPS
     for e in range(width):
@@ -130,9 +130,7 @@
     pair,
     scale,
     spread,
-    wide,
     chains,
-    keeps,
 ):
     seqs, size, depth = x.shape
     rows = couple.shape[0]
@@ -161,7 +159,7 @@
         present[s] = jnp.broadcast_to(to_column(row, size), (size, LANES))
         row_pieces.append(row)
     present_row[...] = jnp.concatenate(row_pieces, axis=1)
-    prepare(ids_row, amino_row, emb, couple, presence, reduce, pair, scale, spread, wide, chains, keeps)
+    prepare(ids_row, amino_row, emb, couple, presence, reduce, pair, scale, spread, chains)
 
 
 def attend(order, bias, scores, content, gate, present, present_row, x, merge, twin, mixed, out):
@@ -257,13 +255,11 @@
     gate,
     present,
     present_row,
-    wide,
     chains,
-    keeps,
 ):
     kept = (scores, content, gate, present, present_row)
     project(
-        x, weights, presence, ids_row, amino_row, emb, couple, reduce, *kept, pair, scale, spread, wide, chains, keeps
+        x, weights, presence, ids_row, amino_row, emb, couple, reduce, *kept, pair, scale, spread, chains
     )
     attend(order, bias, *kept, x, merge, twin, mixed, out)
 
@@ -277,12 +273,12 @@
     groups = spread.shape[0] // width
     blocks = right_rows.shape[0]
     seqs = blocks * LANES // size
-    for slot, peer in enumerate(order):
-        for block in range(blocks):
-            right_rows[block, pl.ds(peer, width, stride=devices), :] = got[
-                slot, block * width : (block + 1) * width, :
-            ].astype(F32)
-        left_rows[pl.ds(peer, seqs * rows, stride=devices), :] = got[slot, blocks * width :, :].astype(F32)
+    inverse = [order.index(peer) for peer in range(devices)]
+    for block in range(blocks):
+        mine = jnp.stack([got[slot, block * width : (block + 1) * width, :].astype(F32) for slot in inverse])
+        right_rows[block] = jnp.swapaxes(mine, 0, 1).reshape(width * devices, LANES)
+    mine = jnp.stack([got[slot, blocks * width :, :].astype(F32) for slot in inverse])
+    left_rows[...] = jnp.swapaxes(mine, 0, 1).reshape(left_rows.shape)
     right = jnp.concatenate([jnp.transpose(right_rows[block]) for block in range(blocks)], axis=0).astype(BF16)
     copies = LANES // width
     tiles = groups // copies
@@ -415,8 +411,6 @@
             pltpu.VMEM((seqs, size, merged), F32),
             pltpu.VMEM((seqs, size, LANES), F32),
             pltpu.VMEM((1, seqs * size), F32),
-            pltpu.VMEM((width * width, channels), F32),
-            pltpu.VMEM((size, channels), F32),
             pltpu.VMEM((size, channels), F32),
         ],
     )(bias, x, weights, presence, ids_row, amino_row, emb, couple, reduce, merge, twin)

time: 24.6 us -> 24.7 us (level)
  no operation moved by 1% of the time
where the time goes in v7:
time: 24.7 us; the launch traced here: 24.5 us
  blocking collectives  19.6 us (79%)
  Pallas kernels  4.16 us (17%)
  between operations  0.65 us (3%)
    all_to_all x1, blocking collectives, on_device(): bias = lax.all_to_all(bias, 'dap', 0, 0, axis_index_groups=[order])  11 us
    all_to_all x1, blocking collectives, on_device(): factors = lax.all_to_all(factors, 'dap', 0, 0, axis_index_groups=[order])  8.63 us
    pallas_call x1, Pallas kernels, on_device(): call(bias_kernel, (struct((devices, size // pack, LANES), BF16),) + tuple...  1.49 us
    pallas_call x1, Pallas kernels, on_device(): call(functools.partial(middle_kernel, order), (pltpu.VMEM(alignment_featu...  1.4 us
    pallas_call x1, Pallas kernels, on_device(): pl.pallas_call(functools.partial(outer_kernel, order), out_shape=(struct(...  1.28 us

profile of v7, /device:TPU:0, one launch (start us, length us, event | category | flops | bytes accessed | tf_op | source)
XLA Modules:
  0.0 24.5 jit_solution(14133788266371206652)
XLA Ops:
  0.6 1.5 %pair_bias.1 = (bf16[8,32,128]{2,1,0:T(8,128)(2,1)S(1)}, bf16[8,64,128]{2,1,0:T(8,128)(2,1)S(1)}, s32[1,64]{1,0:T(1,128)S(1)}, f32[2,128]{1,0:T(2,128)S(1)}, bf1...) custom-call(bf16[8,64,128]{2,1,0:T(8,128)(2,1)} %refs_0_.1, ...), custom_call_target="tpu_custom_call" | custom-call | flops 16777216 | bytes 131072 | tf_op jit(solution)/shard_map/pair_bias/pallas_call | solution.py:378
  2.1 11.0 %all_to_all.10.bias = bf16[8,32,128]{2,1,0:T(8,128)(2,1)S(1)} all-to-all(bf16[8,32,128]{2,1,0:T(8,128)(2,1)S(1)} %get-tuple-element.20), channel_id=1, replica_groups={{5,4,3,2,1,0,7,6},{13,12,11,10,9,8,15,14},{21,20,19,18,17,16,23,22},{29..., dimensions={0} | all-to-all | bytes 131072 | tf_op jit(solution)/shard_map/all_to_all | solution.py:392
  13.2 1.4 %attend.1 = (bf16[2,64,256]{2,1,0:T(8,128)(2,1)S(1)}, bf16[8,48,128]{2,1,0:T(8,128)(2,1)S(1)}, f32[8,64,128]{2,1,0:T(8,128)S(1)}, f32[8,64,128]{2,1,0:T(8,128)S(1)}, bf16[256,512]{1,0:T(8,128)(2,1)S(1)}) custom-call(bf16[8,32,128]{2,1,0:T(8,128)(2,1)S(1)} %all_to_all.10.bias, bf16[2,64,256]{2,1,0:T(8,128)(2,1)S(1)} %get-tuple-element.21.x, ...), custom_call_target="tpu_custom_call" | custom-call | flops 167772160 | bytes 1048576 | tf_op jit(solution)/shard_map/attend/pallas_call | solution.py:395
  14.6 8.6 %all_to_all.11.got = bf16[8,48,128]{2,1,0:T(8,128)(2,1)S(1)} all-to-all(bf16[8,48,128]{2,1,0:T(8,128)(2,1)S(1)} %get-tuple-element.31), channel_id=1, replica_groups={{5,4,3,2,1,0,7,6},{13,12,11,10,9,8,15,14},{21,20,19,18,17,16,23,22},{29..., dimensions={0} | all-to-all | bytes 196608 | tf_op jit(solution)/shard_map/all_to_all | solution.py:417
  23.2 1.3 %outer_mean.1 = (bf16[8,64,128]{2,1,0:T(8,128)(2,1)}, bf16[2,64,256]{2,1,0:T(8,128)(2,1)}) custom-call(bf16[8,48,128]{2,1,0:T(8,128)(2,1)S(1)} %all_to_all.11.got, bf16[256,512]{1,0:T(8,128)(2,1)S(1)} %get-tuple-element.32.spread, f32[8,64,128]{2,1,0:T(8,128)S(1)} %get-tuple-element.33.pair, f32[8,64,128]{2,1,0:T(8,128)S(1)} %get-tuple-element.34.scale, ...), custom_call_target="tpu_custom_call" | custom-call | flops 134217728 | bytes 1048576 | tf_op jit(solution)/shard_map/outer_mean/pallas_call | solution.py:419
